TPU v7x, 32 devices: a whole 2x2x4 slice. The times are simulated.
32 devices in a mesh: dp: 2 (over y), row: 4 (over z), col: 4 (over x, core).
Axes of the slice: x: 2, y: 2, z: 4, core: 2. Of those that a mesh axis runs over, the one named last changes fastest.
Arguments:
- inputs: bfloat16 [2, 256, 128, 512], P('dp', None, 'row', 'col'), may hold values from -6 to 6
- reduce_weight: bfloat16 [64, 256], replicated, may hold values from -0.375 to 0.375
- spatial_weight: bfloat16 [3, 3, 64, 64], replicated, may hold values from -0.25 to 0.25
- expand_weight: bfloat16 [256, 64], replicated, may hold values from -0.75 to 0.75
- class_weight: bfloat16 [3, 3, 135, 256], replicated, may hold values from -0.125 to 0.125
- anchor_labels: int32 [2, 9, 128, 512], P('dp', None, 'row', 'col'), may hold values from 0 to 15, as said below
- anchor_mask: int32 [2, 9, 128, 512], P('dp', None, 'row', 'col'), may hold values from 0 to 1, as said below
Outputs:
- loss: float32 [], replicated
- grad_reduce: float32 [64, 256], replicated
- grad_spatial: float32 [3, 3, 64, 64], replicated
- grad_expand: float32 [256, 64], replicated
- grad_class: float32 [3, 3, 135, 256], replicated
Inputs may be any that keep to these rules, and one draw needn't show every extreme that they name: `anchor_labels`: labels are 0 to 15; anchor 0 at the first row and column of every tile is positive. `anchor_mask`: every anchor with a label above 0 has mask 1.
All inputs are finite; a program needn't handle non-finite values.
Results may differ from a plain program's by a relative error of at most 0.0034.
Values may be sent and summed in bfloat16 or wider, within the bound.
A program may use at most 128 MiB of HBM per device.

v0:
```python
import functools

import jax
import jax.numpy as jnp
import numpy as np
from jax import lax
from jax.experimental import pallas as pl
from jax.experimental.pallas import tpu as pltpu
from jax.sharding import PartitionSpec as P

A = 9
K = 15
HALO = 4
STEP = 512
EDGE = 256
F32 = jnp.float32
BF16 = jnp.bfloat16
AXES = ("dp", "row", "col")


def row_of(mid_ref, top_ref, low_ref, h):
    rows = mid_ref.shape[0]
    if h < HALO:
        return top_ref[h]
    if h < HALO + rows:
        return mid_ref[h - HALO]
    return low_ref[h - HALO - rows]


def halo_kernel(
    sizes, mid_ref, top_ref, low_ref, left_ref, right_ref,
    got_top, got_low, send_left, send_right, got_left, got_right, ssem, rsem,
):
    rows, _, cols = mid_ref.shape
    tall = rows + 2 * HALO
    me = {axis: lax.axis_index(axis) for axis in ("row", "col")}
    mesh_id = pl.DeviceIdType.MESH
    sides = [(axis, step) for axis in ("row", "col") for step in (1, -1)]

    def exists(axis, step):
        return me[axis] < sizes[axis] - 1 if step > 0 else me[axis] > 0

    barrier = pltpu.get_barrier_semaphore()
    for axis, step in sides:
        @pl.when(exists(axis, step))
        def _():
            pl.semaphore_signal(
                barrier, inc=1, device_id={axis: me[axis] + step}, device_id_type=mesh_id
            )
    peers = sum(jnp.where(exists(axis, step), 1, 0) for axis, step in sides)
    pl.semaphore_wait(barrier, peers)

    def push(n, src, dst, axis, step):
        copy = pltpu.make_async_remote_copy(
            src_ref=src, dst_ref=dst, send_sem=ssem.at[n], recv_sem=rsem.at[n],
            device_id={axis: me[axis] + step}, device_id_type=mesh_id,
        )

        @pl.when(exists(axis, step))
        def _():
            copy.start()

        def finish():
            @pl.when(exists(axis, step))
            def _():
                copy.wait_send()

            @pl.when(exists(axis, -step))
            def _():
                copy.wait_recv()

            @pl.when(jnp.logical_not(exists(axis, -step)))
            def _():
                dst[...] = jnp.zeros(dst.shape, dst.dtype)

        return finish

    down = push(0, mid_ref.at[pl.ds(rows - HALO, HALO)], got_top, "row", 1)
    up = push(1, mid_ref.at[pl.ds(0, HALO)], got_low, "row", -1)

    def pack(h):
        cells = row_of(mid_ref, got_top, got_low, h)
        send_left[:, h * HALO:(h + 1) * HALO] = cells[:, :HALO]
        send_right[:, h * HALO:(h + 1) * HALO] = cells[:, cols - HALO:]

    send_left[...] = jnp.zeros_like(send_left)
    send_right[...] = jnp.zeros_like(send_right)
    for h in range(HALO, HALO + rows):
        pack(h)
    down()
    up()
    for h in list(range(HALO)) + list(range(HALO + rows, tall)):
        pack(h)
    forth = push(2, send_right, got_left, "col", 1)
    back = push(3, send_left, got_right, "col", -1)
    top_ref[...] = got_top[...]
    low_ref[...] = got_low[...]
    forth()
    back()
    left_ref[...] = got_left[...]
    right_ref[...] = got_right[...]


def halos(field):
    rows, depth, cols = field.shape
    sizes = {axis: lax.axis_size(axis) for axis in ("row", "col")}
    lanes = -(-(rows + 2 * HALO) * HALO // 128) * 128
    band, strip = (HALO, depth, cols), (depth, lanes)
    return pl.pallas_call(
        functools.partial(halo_kernel, sizes),
        out_shape=[jax.ShapeDtypeStruct(v, BF16) for v in (band, band, strip, strip)],
        in_specs=[pl.BlockSpec(memory_space=pltpu.VMEM)],
        out_specs=[pl.BlockSpec(memory_space=pltpu.VMEM)] * 4,
        scratch_shapes=[pltpu.VMEM(v, BF16) for v in (band, band, strip, strip, strip, strip)]
        + [pltpu.SemaphoreType.DMA((4,)), pltpu.SemaphoreType.DMA((4,))],
        compiler_params=pltpu.CompilerParams(
            collective_id=1, has_side_effects=True, vmem_limit_bytes=16 * 1024 * 1024
        ),
        name="halos",
    )(field)


def dot(a, b):
    return jnp.dot(a, b, preferred_element_type=F32)


def dot_t(a, b):
    return lax.dot_general(a, b, (((1,), (1,)), ((), ())), preferred_element_type=F32)


def tile_kernel(
    pitch, geo, heads_in,
    mid_ref, top_ref, low_ref, left_ref, right_ref, own_ref, spread_ref, wr_ref, ws_ref, wsb_ref, we_ref, wet_ref, wc_ref, wcb_ref,
    pack_ref, stat_ref,
    x_ref, first, second, block, dlog, dsec, big, small, acc_c, reduce_ref, spatial_ref, expand_ref,
):
    chans = we_ref.shape[0]
    mid = we_ref.shape[1]
    outs = wc_ref.shape[0]
    length = x_ref.shape[1]
    shifts = [(dy - 1) * pitch + (dx - 1) for dy in range(3) for dx in range(3)]

    def columns(ref, base, sign, dest):
        rows = ref.shape[0]
        window = ref[:, pl.ds(base, STEP + 2 * EDGE)]
        for tap, shift in enumerate(shifts):
            at = EDGE + sign * shift
            dest[tap * rows:(tap + 1) * rows, :] = window[:, at:at + STEP]

    def at(i, start):
        return pl.multiple_of(start + i * STEP, 128)

    def loop(start, steps, body, init=0):
        return lax.fori_loop(0, steps, lambda i, c: body(at(i, start), c), init)

    rows, _, cols = mid_ref.shape
    tall = rows + 2 * HALO
    x_ref[:, tall * pitch // 128 * 128:] = jnp.zeros(
        (x_ref.shape[0], length - tall * pitch // 128 * 128), BF16
    )
    for h in range(tall):
        x_ref[:, h * pitch:h * pitch + HALO] = left_ref[:, h * HALO:(h + 1) * HALO]
        x_ref[:, h * pitch + HALO:h * pitch + HALO + cols] = row_of(
            mid_ref, top_ref, low_ref, h
        )
        x_ref[:, h * pitch + HALO + cols:(h + 1) * pitch] = right_ref[:, h * HALO:(h + 1) * HALO]

    first[:, :EDGE] = jnp.zeros((mid, EDGE), BF16)
    first[:, EDGE + length:] = jnp.zeros((mid, EDGE), BF16)
    dlog[...] = jnp.zeros_like(dlog)
    acc_c[...] = jnp.zeros_like(acc_c)
    reduce_ref[...] = jnp.zeros_like(reduce_ref)
    spatial_ref[...] = jnp.zeros_like(spatial_ref)
    expand_ref[...] = jnp.zeros_like(expand_ref)

    def make_first(p, c):
        z = dot(wr_ref[...], x_ref[:chans, pl.ds(p, STEP)])
        first[:, pl.ds(pl.multiple_of(p + EDGE, 128), STEP)] = jnp.maximum(z, 0.0).astype(BF16)
        return c

    loop(0, length // STEP, make_first)

    def make_block(p, c):
        columns(first, p, 1, small)
        s = jnp.maximum(dot(ws_ref[...], small[...]), 0.0).astype(BF16)
        second[:, pl.ds(p, STEP)] = s
        xs = x_ref[:, pl.ds(p, STEP)]
        valid = xs[chans + A:chans + A + 1].astype(F32)
        b = jnp.maximum(xs[:chans].astype(F32) + dot(we_ref[...], s), 0.0) * valid
        block[:, pl.ds(p, STEP)] = b.astype(BF16)
        return c

    loop(0, length // STEP, make_block)

    ident = lax.rem(lax.broadcasted_iota(jnp.int32, (outs, 1), 0), K) + 1

    def make_dlog(p, carry):
        total, count = carry
        columns(block, pl.multiple_of(p - EDGE, 128), 1, big)
        z = dot(wc_ref[...], big[...])
        code = x_ref[chans:, pl.ds(p, STEP)]
        own = own_ref[:, pl.ds(p, STEP)]
        wide = dot(spread_ref[...], code)
        live = wide >= 15.5
        label = jnp.where(live, wide - 16.0, wide)
        target = label == ident.astype(F32)
        alpha = jnp.where(target, 0.25, 0.75)
        alpha = jnp.where(live, alpha, 0.0)
        u = jnp.where(target, -z, z)
        e = jnp.exp(-jnp.abs(u))
        inv = 1.0 / (1.0 + e)
        low = e * inv
        pos = u >= 0.0
        prob = jnp.where(pos, inv, low)
        rest = jnp.where(pos, low, inv)
        soft = jnp.maximum(u, 0.0) + jnp.log1p(e)
        scaled = alpha * prob * prob
        total = total + jnp.sum(scaled * soft, axis=0, keepdims=True) * own
        slope = scaled * (2.0 * rest * soft + prob)
        d = jnp.where(target, -slope, slope).astype(BF16)
        dlog[:, pl.ds(p, STEP)] = d
        mine = (d.astype(F32) * own).astype(BF16)
        acc_c[...] += dot_t(mine, big[...])
        codes = code.astype(F32)
        labels = jnp.where(codes >= 15.5, codes - 16.0, codes)
        row = lax.broadcasted_iota(jnp.int32, codes.shape, 0)
        hit = jnp.where((labels > 0.5) & (row < A), 1.0, 0.0)
        count = count + jnp.sum(hit, axis=0, keepdims=True) * own
        return total, count

    zero = jnp.zeros((1, STEP), F32)
    total, count = loop(geo[0][0], geo[0][1], make_dlog, (zero, zero))
    stat_ref[0:1, :] = sum(total[:, k * 128:(k + 1) * 128] for k in range(STEP // 128))
    stat_ref[1:2, :] = sum(count[:, k * 128:(k + 1) * 128] for k in range(STEP // 128))
    stat_ref[2:, :] = jnp.zeros((6, 128), F32)

    def make_dsec(p, c):
        columns(dlog, pl.multiple_of(p - EDGE, 128), -1, big.at[:9 * outs])
        g = dot(wcb_ref[...], big[:9 * outs, :])
        b = block[:, pl.ds(p, STEP)].astype(F32)
        ds = jnp.where(b > 0.0, g, 0.0).astype(BF16)
        s = second[:, pl.ds(p, STEP)]
        own = own_ref[:, pl.ds(p, STEP)]
        sf = s.astype(F32)
        expand_ref[...] += dot_t((sf * own).astype(BF16), ds)
        h = dot(wet_ref[...], ds)
        dsec[:, pl.ds(p, STEP)] = jnp.where(sf > 0.0, h, 0.0).astype(BF16)
        return c

    loop(geo[0][0], geo[0][1], make_dsec)

    def make_dfirst(p, c):
        own = own_ref[:, pl.ds(p, STEP)]
        columns(first, p, 1, small)
        mine = (dsec[:, pl.ds(p, STEP)].astype(F32) * own).astype(BF16)
        spatial_ref[...] += dot_t(mine, small[...])
        columns(dsec, pl.multiple_of(p - EDGE, 128), -1, small)
        g = dot(wsb_ref[...], small[...]) * own
        f = first[:, pl.ds(pl.multiple_of(p + EDGE, 128), STEP)].astype(F32)
        df = jnp.where(f > 0.0, g, 0.0).astype(BF16)
        reduce_ref[...] += dot_t(df, x_ref[:chans, pl.ds(p, STEP)])
        return c

    loop(geo[1][0], geo[1][1], make_dfirst)
    heads = heads_in
    spots = layout(mid, heads)[:3]
    pack_ref[...] = jnp.zeros_like(pack_ref)
    for tap in range(9):
        pack_ref[tap * heads:(tap + 1) * heads, :] = acc_c[:heads, tap * chans:(tap + 1) * chans]
    pack_ref[spots[0]:spots[0] + mid, :] = reduce_ref[...]
    pack_ref[spots[1]:spots[1] + mid, :] = expand_ref[...]
    for dy in range(3):
        at_row = spots[2] + dy * mid
        pack_ref[at_row:at_row + mid, :3 * mid] = spatial_ref[:, dy * 3 * mid:(dy + 1) * 3 * mid]


def layout(mid, heads):
    first = -(-9 * heads // 8) * 8
    return first, first + mid, first + 2 * mid, first + 5 * mid


def piece_rows(s, orders, sizes, total):
    rows, out = total // len(orders), []
    for axis in orders[s]:
        rows //= sizes[axis]
        out.append(rows)
    return out


def sum_kernel(sizes, orders, pack_ref, stat_ref, out_ref, total_ref, *scratch):
    subs, depth = len(orders), len(AXES)
    send, full = scratch[0], scratch[1]
    recvs = [scratch[2 + s * depth:2 + (s + 1) * depth] for s in range(subs)]
    stat_send = scratch[2 + subs * depth]
    stat_recv = scratch[3 + subs * depth:3 + subs * depth + depth]
    ssem, rsem = scratch[-2:]
    total = pack_ref.shape[0]
    share = total // subs
    me = {axis: lax.axis_index(axis) for axis in AXES}
    peers = lambda axis: range(1, sizes[axis])
    mesh_id = pl.DeviceIdType.MESH

    barrier = pltpu.get_barrier_semaphore()
    for axis in AXES:
        for d in peers(axis):
            pl.semaphore_signal(
                barrier, inc=1, device_id={axis: lax.rem(me[axis] + d, sizes[axis])},
                device_id_type=mesh_id,
            )
    pl.semaphore_wait(barrier, sum(sizes[axis] - 1 for axis in AXES))

    used = [0]

    def push(src, dst, axis, d):
        n = used[0]
        used[0] += 1
        copy = pltpu.make_async_remote_copy(
            src_ref=src, dst_ref=dst, send_sem=ssem.at[n], recv_sem=rsem.at[n],
            device_id={axis: lax.rem(me[axis] + d, sizes[axis])}, device_id_type=mesh_id,
        )
        copy.start()
        return copy

    send[...] = pack_ref[...].astype(BF16)
    base = [s * share for s in range(subs)]
    held = [None] * subs
    stat = stat_ref[...]
    for k in range(depth):
        copies = []
        for s in range(subs):
            axis = orders[s][k]
            rows = piece_rows(s, orders, sizes, total)[k]
            for d in peers(axis):
                to = lax.rem(me[axis] + d, sizes[axis])
                src = send.at[pl.ds(pl.multiple_of(base[s] + to * rows, 16), rows)]
                copies.append(push(src, recvs[s][k].at[d - 1], axis, d))
        stat_send[k] = stat
        for d in peers(AXES[k]):
            copies.append(push(stat_send.at[k], stat_recv[k].at[d - 1], AXES[k], d))
        for copy in copies:
            copy.wait()
        for d in peers(AXES[k]):
            stat = stat + stat_recv[k][d - 1]
        for s in range(subs):
            axis = orders[s][k]
            rows = piece_rows(s, orders, sizes, total)[k]
            mine = me[axis] * rows
            if k == 0:
                got = pack_ref[pl.ds(pl.multiple_of(base[s] + mine, 16), rows), :]
            else:
                out_at = pl.ds(pl.multiple_of(base[s] + mine, 16), rows)
                got = out_ref[out_at, :]
            for d in peers(axis):
                got = got + recvs[s][k][d - 1].astype(F32)
            base[s] = pl.multiple_of(base[s] + mine, 16)
            where = pl.ds(base[s], rows)
            if k < depth - 1:
                out_ref[where, :] = got
                send[where, :] = got.astype(BF16)
            else:
                full[where, :] = got.astype(BF16)
    total_ref[...] = stat
    for k in range(depth - 1, -1, -1):
        copies = []
        for s in range(subs):
            axis = orders[s][k]
            rows = piece_rows(s, orders, sizes, total)[k]
            where = pl.ds(base[s], rows)
            for d in peers(axis):
                copies.append(push(full.at[where], full.at[where], axis, d))
            base[s] = pl.multiple_of(base[s] - me[axis] * rows, 16)
        for copy in copies:
            copy.wait()
    out_ref[...] = full[...].astype(F32)


def sum_devices(pack, stat):
    sizes = {axis: lax.axis_size(axis) for axis in AXES}
    orders = [AXES[s:] + AXES[:s] for s in range(len(AXES))]
    total, chans = pack.shape
    scratch = [pltpu.VMEM((total, chans), BF16), pltpu.VMEM((total, chans), BF16)]
    copies = 0
    for s in range(len(orders)):
        for axis, rows in zip(orders[s], piece_rows(s, orders, sizes, total)):
            scratch.append(pltpu.VMEM((max(sizes[axis] - 1, 1), rows, chans), BF16))
            copies += 2 * (sizes[axis] - 1)
    scratch.append(pltpu.VMEM((len(AXES),) + stat.shape, F32))
    for axis in AXES:
        scratch.append(pltpu.VMEM((max(sizes[axis] - 1, 1),) + stat.shape, F32))
        copies += sizes[axis] - 1
    scratch += [pltpu.SemaphoreType.DMA((copies,)), pltpu.SemaphoreType.DMA((copies,))]
    return pl.pallas_call(
        functools.partial(sum_kernel, sizes, orders),
        out_shape=(
            jax.ShapeDtypeStruct(pack.shape, F32), jax.ShapeDtypeStruct(stat.shape, F32)
        ),
        in_specs=[pl.BlockSpec(memory_space=pltpu.VMEM)] * 2,
        out_specs=[pl.BlockSpec(memory_space=pltpu.VMEM)] * 2,
        scratch_shapes=scratch,
        compiler_params=pltpu.CompilerParams(
            collective_id=0, has_side_effects=True, vmem_limit_bytes=16 * 1024 * 1024
        ),
        name="sum_devices",
    )(pack, stat)


def per_device(
    inputs, reduce_weight, spatial_weight, expand_weight, class_weight, anchor_labels, anchor_mask
):
    tiles, chans, rows, cols = inputs.shape
    mid = reduce_weight.shape[0]
    heads = class_weight.shape[2]
    outs = -(-heads // 16) * 16
    tall, pitch = rows + 2 * HALO, cols + 2 * HALO
    pixels = tall * pitch
    length = -(-pixels // STEP) * STEP

    def span(margin):
        low = margin * pitch + margin
        high = (tall - margin) * pitch
        start = max(EDGE, low // 128 * 128 // EDGE * EDGE)
        return start, -(-(high - start) // STEP)

    geo = (span(2), span(4))
    need = geo[0][0] + geo[0][1] * STEP + EDGE
    length = max(length, -(-need // STEP) * STEP)

    code = (anchor_labels + 16 * anchor_mask).astype(BF16)
    ones = jnp.ones((tiles, 1, rows, cols), BF16)
    none = jnp.zeros((tiles, 16 - A - 1, rows, cols), BF16)
    field = jnp.concatenate([inputs, code, ones, none], axis=1)
    field = field.transpose(0, 2, 1, 3)

    own = np.zeros((tall, pitch), np.float32)
    own[HALO:HALO + rows, HALO:HALO + cols] = 1.0
    own = jnp.asarray(np.pad(own.reshape(1, pixels), ((0, 0), (0, length - pixels))))
    spread = np.zeros((outs, 16), np.float32)
    spread[np.arange(heads), np.arange(heads) // K] = 1.0
    spread = jnp.asarray(spread, BF16)

    ws = spatial_weight.transpose(2, 0, 1, 3).reshape(mid, 9 * mid)
    wsb = spatial_weight.transpose(3, 0, 1, 2).reshape(mid, 9 * mid)
    wide = jnp.pad(class_weight, ((0, 0), (0, 0), (0, outs - heads), (0, 0)))
    wc = wide.transpose(2, 0, 1, 3).reshape(outs, 9 * chans)
    wcb = wide.transpose(3, 0, 1, 2).reshape(chans, 9 * outs)

    unit = 16 * len(AXES) * int(np.prod([lax.axis_size(axis) for axis in AXES]))
    packed = -(-layout(mid, heads)[3] // unit) * unit

    call = pl.pallas_call(
        functools.partial(tile_kernel, pitch, geo, heads),
        out_shape=(
            jax.ShapeDtypeStruct((packed, chans), F32),
            jax.ShapeDtypeStruct((8, 128), F32),
        ),
        in_specs=[pl.BlockSpec(memory_space=pltpu.VMEM)] * 14,
        out_specs=[pl.BlockSpec(memory_space=pltpu.VMEM)] * 2,
        scratch_shapes=[
            pltpu.VMEM((chans + 16, length), BF16),
            pltpu.VMEM((mid, length + 2 * EDGE), BF16),
            pltpu.VMEM((mid, length), BF16),
            pltpu.VMEM((chans, length), BF16),
            pltpu.VMEM((outs, length), BF16),
            pltpu.VMEM((mid, length), BF16),
            pltpu.VMEM((9 * chans, STEP), BF16),
            pltpu.VMEM((9 * mid, STEP), BF16),
            pltpu.VMEM((outs, 9 * chans), F32),
            pltpu.VMEM((mid, chans), F32),
            pltpu.VMEM((mid, 9 * mid), F32),
            pltpu.VMEM((mid, chans), F32),
        ],
        compiler_params=pltpu.CompilerParams(vmem_limit_bytes=50 * 1024 * 1024),
        name="tile_step",
    )
    sums = None
    for t in range(tiles):
        part = call(
            field[t], *halos(field[t]), own, spread, reduce_weight, ws, wsb, expand_weight, expand_weight.T, wc, wcb
        )
        sums = part if sums is None else tuple(a + b for a, b in zip(sums, part))
    return finish(sums, mid, heads)


def finish(sums, mid, heads):
    pack, stat = sum_devices(*sums)
    chans = pack.shape[1]
    spots = layout(mid, heads)
    count = jnp.sum(stat[1])
    scale = 1.0 / count
    spatial = pack[spots[2]:spots[3], :3 * mid].reshape(3, mid, 3, mid).transpose(0, 2, 1, 3)
    return (
        jnp.sum(stat[0]) / count,
        pack[spots[0]:spots[1]] * scale,
        spatial * scale,
        pack[spots[1]:spots[2]].T * scale,
        pack[:9 * heads].reshape(3, 3, heads, chans) * scale,
    )


def solution(mesh):
    tiled = P("dp", None, "row", "col")
    return jax.shard_map(
        per_device,
        mesh=mesh,
        in_specs=(tiled, P(), P(), P(), P(), tiled, tiled),
        out_specs=(P(), P(), P(), P(), P()),
        check_vma=False,
    )
```

profile of v0, /device:TPU:0, one launch (start us, length us, event | category | flops | bytes accessed | tf_op | source)
XLA Modules:
  0.0 124.6 jit_solution(6426291032104191624)
XLA Ops:
  0.6 0.1 pad.8.clone
  0.7 0.1 pad.7.clone
  0.8 0.9 copy.41.we_ref
  1.7 1.0 copy.40.wsb_ref
  2.7 1.2 fusion
  3.9 1.0 copy.37
  4.9 0.1 copy.39.ws_ref
  5.1 1.2 fusion.1
  6.2 0.3 copy.42.wcb_ref
  6.6 0.5 copy.38
  7.1 0.8 reshape.30.wc_ref
  7.9 2.4 %copy.36 = bf16[1,256,32,128]{3,1,2,0:T(8,128)(2,1)S(1)} copy(bf16[1,256,32,128]{3,2,1,0:T(8,128)(2,1)} %param.9) | data formatting | bytes 4194304 | tf_op args[0]
  10.3 0.6 maximum_bitcast_fusion.mid_ref
  10.9 0.0 copy-start
  10.9 0.0 copy-start.2
  10.9 0.0 copy-start.3
  11.0 0.0 copy-start.4
  11.0 0.0 copy-start.5
  11.0 13.4 %halos.1 = (bf16[4,272,128]{2,1,0:T(8,128)(2,1)S(1)}, bf16[4,272,128]{2,1,0:T(8,128)(2,1)S(1)}, bf16[272,256]{1,0:T(8,128)(2,1)S(1)}, bf16[272,256]{1,0:T(8,128)(2,1)S(1)}) custom-call(bf16[32,272,128]{2,1,0:T(8,128)(2,1)S(1)} %maximum_bitcast_fusion.mid_ref), custom_call_target="tpu_custom_call" | custom-call | tf_op jit(solution)/shard_map/halos/pallas_call | solution.py:109
  24.4 0.0 copy-done
  24.4 0.0 copy-done.2
  24.4 0.0 copy-done.3
  24.5 0.0 copy-done.4
  24.5 0.0 copy-done.5
  24.5 57.0 %tile_step.1 = (f32[1536,256]{1,0:T(8,128)}, f32[8,128]{1,0:T(8,128)S(1)}) custom-call(bf16[32,272,128]{2,1,0:T(8,128)(2,1)} %copy-done, bf16[4,272,128]{2,1,0:T(8,128)(2,1)S(1)} %get-tuple-element.13.top_ref, bf16[4,272,128]{2,1,0:T(8,128)(2,1)S(1)} %get-tuple-element.14.low_ref, bf16[272,256]{1,0:T(8,128)(2,1)S(1)} %get-tuple-element.15.left_ref, ...), custom_call_target="tpu_custom_call" | custom-call | tf_op jit(solution)/shard_map/tile_step/pallas_call | solution.py:477
  81.5 0.0 copy-start.1
  81.5 1.4 %copy-done.1 = f32[1536,256]{1,0:T(8,128)S(1)} copy-done((f32[1536,256]{1,0:T(8,128)S(1)}, f32[1536,256]{1,0:T(8,128)}, u32[]{:S(2)}) %copy-start.1) | copy-done | bytes 1572888
  82.9 35.0 %sum_devices.1 = (f32[1536,256]{1,0:T(8,128)S(1)}, f32[8,128]{1,0:T(8,128)S(1)}) custom-call(f32[1536,256]{1,0:T(8,128)S(1)} %copy-done.1, f32[8,128]{1,0:T(8,128)S(1)} %get-tuple-element.18.stat_ref), custom_call_target="tpu_custom_call" | custom-call | tf_op jit(solution)/shard_map/sum_devices/pallas_call | solution.py:392
  118.0 0.6 slice_reduce_fusion
  120.6 0.7 multiply_bitcast_fusion
  121.3 0.1 slice_multiply_fusion
  121.4 1.2 mul.52
  122.5 0.2 mul.46
  122.7 0.7 copy.43
  (2 shorter events, 0.0 us)
Async XLA Ops:
  10.9 13.5 %copy-start = (bf16[32,272,128]{2,1,0:T(8,128)(2,1)}, bf16[32,272,128]{2,1,0:T(8,128)(2,1)S(1)}, u32[]{:S(2)}) copy-start(bf16[32,272,128]{2,1,0:T(8,128)(2,1)S(1)} %maximum_bitcast_fusion.mid_ref) | copy-start | bytes 6684676
  10.9 13.5 %copy-start.2 = (bf16[256,64]{0,1:T(8,128)(2,1)S(1)}, bf16[256,64]{0,1:T(8,128)(2,1)}, u32[]{:S(2)}) copy-start(bf16[256,64]{0,1:T(8,128)(2,1)} %param.12) | copy-start | bytes 98308
  10.9 13.5 %copy-start.3 = (bf16[144,16]{1,0:T(8,128)(2,1)S(1)}, bf16[144,16]{1,0:T(8,128)(2,1)}, u32[]{:S(2)}) copy-start(bf16[144,16]{1,0:T(8,128)(2,1)} %constant.17.clone.spread_ref) | copy-start | bytes 13828
  11.0 13.5 %copy-start.4 = (bf16[64,256]{1,0:T(8,128)(2,1)S(1)}, bf16[64,256]{1,0:T(8,128)(2,1)}, u32[]{:S(2)}) copy-start(bf16[64,256]{1,0:T(8,128)(2,1)} %wr_ref.1) | copy-start | bytes 98308
  11.0 13.5 %copy-start.5 = (f32[1,5632]{1,0:T(1,128)S(1)}, f32[1,5632]{1,0:T(1,128)}, u32[]{:S(2)}) copy-start(f32[1,5632]{1,0:T(1,128)} %constant.16.clone.own_ref) | copy-start | bytes 67588
  81.5 1.4 %copy-start.1 = (f32[1536,256]{1,0:T(8,128)S(1)}, f32[1536,256]{1,0:T(8,128)}, u32[]{:S(2)}) copy-start(f32[1536,256]{1,0:T(8,128)} %get-tuple-element.17.pack_ref) | copy-start | bytes 4718596
where the time goes:
time: 125 us
  Pallas kernels  106 us (85%)
  local copies, waits for them, and re-layouts  12 us (10%)
  between operations  3.95 us (3%)
  other arithmetic  3.18 us (3%)
    pallas_call x1, Pallas kernels, per_device(): call(field[t], *halos(field[t]), own, spread, reduce_weight, ws, wsb, exp...  57 us
    pallas_call x1, Pallas kernels, sum_devices(): pl.pallas_call(functools.partial(sum_kernel, sizes, orders), out_shape=(j...  35 us
    pallas_call x1, Pallas kernels, halos(): pl.pallas_call(functools.partial(halo_kernel, sizes), out_shape=[jax.Shap...  13.4 us
    unnamed x15, local copies, waits for them, and re-layouts  5.45 us

commit v1 on v0

v1 whole, which is shorter than its diff:
```python
import functools

import jax
import jax.numpy as jnp
import numpy as np
from jax import lax
from jax.experimental import pallas as pl
from jax.experimental.pallas import tpu as pltpu
from jax.sharding import PartitionSpec as P

A = 9
K = 15
GROUP = 4
WIDE = 8
LOG2E = 1.4426950408889634
LN2 = 0.6931471805599453
F32 = jnp.float32
BF16 = jnp.bfloat16
AXES = ("dp", "row", "col")


def dot(a, b):
    return jnp.dot(a, b, preferred_element_type=F32)


def dot_t(a, b):
    return lax.dot_general(a, b, (((1,), (1,)), ((), ())), preferred_element_type=F32)


def step_kernel(
    sizes, heads,
    x_ref, code_ref, spread_ref, wr_ref, ws_ref, wsb_ref, we_ref, wet_ref, wc_ref, wcb_ref,
    pack_ref, stat_ref,
    first, second, block, dlog, dzero, dsec, dsec_zero, acc_c, acc_s, acc_e, acc_r,
    strips, got, ssem, rsem,
):
    rows, chans, cols = x_ref.shape
    mid = wr_ref.shape[0]
    outs = wc_ref.shape[1]
    me = {axis: lax.axis_index(axis) for axis in ("row", "col")}
    mesh_id = pl.DeviceIdType.MESH
    sides = [(axis, step) for axis in ("row", "col") for step in (1, -1)]

    def exists(axis, step):
        return me[axis] < sizes[axis] - 1 if step > 0 else me[axis] > 0

    barrier = pltpu.get_barrier_semaphore()
    for axis, step in sides:
        @pl.when(exists(axis, step))
        def _():
            pl.semaphore_signal(
                barrier, inc=1, device_id={axis: me[axis] + step}, device_id_type=mesh_id
            )

    def push(n, src, dst, axis, step):
        copy = pltpu.make_async_remote_copy(
            src_ref=src, dst_ref=dst, send_sem=ssem.at[n], recv_sem=rsem.at[n],
            device_id={axis: me[axis] + step}, device_id_type=mesh_id,
        )

        @pl.when(exists(axis, step))
        def _():
            copy.start()

        def finish():
            @pl.when(exists(axis, step))
            def _():
                copy.wait_send()

            @pl.when(exists(axis, -step))
            def _():
                copy.wait_recv()

        return finish

    def loop(steps, body, init=0):
        return lax.fori_loop(0, steps, body, init)

    def cat(ref, at, count, low=None, high=None):
        part = slice(low, high)
        return jnp.concatenate([ref[at + k, part, :] for k in range(count)], axis=1)

    def spread_rows(ref, at, value, low=None, high=None):
        for k in range(value.shape[1] // cols):
            ref[at + k, low:high, :] = value[:, k * cols:(k + 1) * cols]

    def clear_edges(n, field, depth):
        blank = jnp.zeros((depth, cols), BF16)

        @pl.when(jnp.logical_not(exists("row", -1)))
        def _():
            field[0, depth:2 * depth, :] = blank

        @pl.when(jnp.logical_not(exists("row", 1)))
        def _():
            field[rows + 1, depth:2 * depth, :] = blank

        for side in range(2):
            @pl.when(jnp.logical_not(exists("col", 1 if side else -1)))
            def _():
                got[n][side] = blank

    def send_rows(n, field, depth):
        down = push(
            4 * n, field.at[rows, pl.ds(depth, depth)], field.at[0, pl.ds(depth, depth)], "row", 1
        )
        up = push(
            4 * n + 1, field.at[1, pl.ds(depth, depth)],
            field.at[rows + 1, pl.ds(depth, depth)], "row", -1,
        )
        return down, up

    def send_strip(n, field, depth, held):
        lane = lax.broadcasted_iota(jnp.int32, (depth, cols), 1)

        def gather(i, strip):
            row = field[i, depth:2 * depth, :]
            return jnp.where(lane // 2 == i, pltpu.roll(row, 2 * i + 1, 1), strip)

        strip = lax.fori_loop(1, rows + 1, gather, jnp.zeros((depth, cols), BF16))
        for wait in held:
            wait()
        strip = gather(rows + 1, gather(0, strip))
        strips[n][...] = strip
        right = push(4 * n + 2, strips[n], got[n].at[0], "col", 1)
        left = push(4 * n + 3, strips[n], got[n].at[1], "col", -1)
        return right, left

    def widen(n, field, depth, held):
        for wait in held:
            wait()
        lane = lax.broadcasted_iota(jnp.int32, (depth, cols), 1)
        before, after = got[n][0], got[n][1]

        def fill(i, c):
            row = field[i, depth:2 * depth, :]
            field[i, :depth, :] = jnp.where(
                lane == 0, pltpu.roll(before, cols - 2 * i, 1), pltpu.roll(row, 1, 1)
            )
            field[i, 2 * depth:, :] = jnp.where(
                lane == cols - 1, pltpu.roll(after, cols - 2 - 2 * i, 1),
                pltpu.roll(row, cols - 1, 1),
            )
            return c

        loop(rows + 2, fill)

    def conv(weight, field, at):
        return sum(dot(weight[dy], cat(field, at + dy, GROUP)) for dy in range(3))

    fields = [(first, mid), (block, chans), (dlog, outs), (dsec, mid)]
    for n, (field, depth) in enumerate(fields):
        clear_edges(n, field, depth)
    for ref in (dzero, dsec_zero):
        ref[0] = jnp.zeros(ref.shape[1:], BF16)
        ref[rows + 1] = jnp.zeros(ref.shape[1:], BF16)
    for ref in (acc_c, acc_s, acc_e, acc_r):
        ref[...] = jnp.zeros_like(ref)
    peers = sum(jnp.where(exists(axis, step), 1, 0) for axis, step in sides)
    pl.semaphore_wait(barrier, peers)

    def make_first(i, c):
        z = dot(wr_ref[...], cat(x_ref, i * GROUP, GROUP))
        spread_rows(first, i * GROUP + 1, jnp.maximum(z, 0.0).astype(BF16), mid, 2 * mid)
        return c

    loop(rows // GROUP, make_first)
    held = send_rows(0, first, mid)
    held = send_strip(0, first, mid, held)
    widen(0, first, mid, held)

    def make_block(i, c):
        s = jnp.maximum(conv(ws_ref, first, i * GROUP), 0.0).astype(BF16)
        spread_rows(second, i * GROUP, s)
        b = jnp.maximum(cat(x_ref, i * GROUP, GROUP).astype(F32) + dot(we_ref[...], s), 0.0)
        spread_rows(block, i * GROUP + 1, b.astype(BF16), chans, 2 * chans)
        return c

    loop(rows // GROUP, make_block)
    held = send_rows(1, block, chans)
    held = send_strip(1, block, chans, held)
    widen(1, block, chans, held)

    def make_dlog(i, carry):
        total, count = carry
        z = conv(wc_ref, block, i * GROUP)
        code = cat(code_ref, i * GROUP, GROUP)
        gap = dot(spread_ref[...], code)
        target = gap == 0.0
        alpha = jnp.where(target, 0.25, jnp.where(gap > 32.0, 0.0, 0.75))
        z = z * LOG2E
        u = jnp.where(target, -z, z)
        e = jnp.exp2(-jnp.abs(u))
        soft = jnp.maximum(u, 0.0) + jnp.log2(1.0 + e)
        prob = jnp.exp2(u - soft)
        scaled = alpha * prob * prob
        total = total + jnp.sum(scaled * soft, axis=0, keepdims=True)
        slope = scaled * ((2.0 * LN2 - 2.0 * LN2 * prob) * soft + prob)
        d = jnp.where(target, -slope, slope).astype(BF16)
        spread_rows(dlog, i * GROUP + 1, d, outs, 2 * outs)
        spread_rows(dzero, i * GROUP + 1, d)
        codes = code.astype(F32)
        row = lax.broadcasted_iota(jnp.int32, codes.shape, 0)
        hit = jnp.where((codes > 0.5) & (codes < 32.0) & (row < A), 1.0, 0.0)
        count = count + jnp.sum(hit, axis=0, keepdims=True)
        return total, count

    zero = jnp.zeros((1, GROUP * cols), F32)
    total, count = loop(rows // GROUP, make_dlog, (zero, zero))
    fold = lambda v: sum(v[:, k * 128:(k + 1) * 128] for k in range(v.shape[1] // 128))
    stat_ref[0:1, :] = fold(total) * LN2
    stat_ref[1:2, :] = fold(count)
    stat_ref[2:, :] = jnp.zeros((6, 128), F32)
    held = send_rows(2, dlog, outs)

    def weight_sum(acc, grad, field):
        depth = grad.shape[1]

        def add(i, c):
            at = i * WIDE + 1
            tall = jnp.concatenate([cat(grad, at + 1 - dy, WIDE) for dy in range(3)], axis=0)
            acc[...] += dot_t(tall, cat(field, at, WIDE))
            return c

        loop(rows // WIDE, add)
        acc[:depth, :] += dot_t(grad[1], field[0])
        acc[2 * depth:, :] += dot_t(grad[rows], field[rows + 1])

    weight_sum(acc_c, dzero, block)
    held = send_strip(2, dlog, outs, held)
    widen(2, dlog, outs, held)

    def make_dsec(i, c):
        g = conv(wcb_ref, dlog, i * GROUP)
        b = cat(block, i * GROUP + 1, GROUP, chans, 2 * chans).astype(F32)
        ds = jnp.where(b > 0.0, g, 0.0).astype(BF16)
        s = cat(second, i * GROUP, GROUP)
        acc_e[...] += dot_t(s, ds)
        h = dot(wet_ref[...], ds)
        d = jnp.where(s.astype(F32) > 0.0, h, 0.0).astype(BF16)
        spread_rows(dsec, i * GROUP + 1, d, mid, 2 * mid)
        spread_rows(dsec_zero, i * GROUP + 1, d)
        return c

    loop(rows // GROUP, make_dsec)
    held = send_rows(3, dsec, mid)
    weight_sum(acc_s, dsec_zero, first)
    held = send_strip(3, dsec, mid, held)
    widen(3, dsec, mid, held)

    def make_dfirst(i, c):
        g = conv(wsb_ref, dsec, i * GROUP)
        f = cat(first, i * GROUP + 1, GROUP, mid, 2 * mid).astype(F32)
        df = jnp.where(f > 0.0, g, 0.0).astype(BF16)
        acc_r[...] += dot_t(df, cat(x_ref, i * GROUP, GROUP))
        return c

    loop(rows // GROUP, make_dfirst)
    spots = layout(mid, heads)[:3]
    pack_ref[9 * heads:, :] = jnp.zeros((pack_ref.shape[0] - 9 * heads, chans), F32)
    for dy in range(3):
        for dx in range(3):
            tap = 3 * dy + dx
            pack_ref[tap * heads:(tap + 1) * heads, :] = acc_c[
                dy * outs:dy * outs + heads, dx * chans:(dx + 1) * chans
            ]
    pack_ref[spots[0]:spots[0] + mid, :] = acc_r[...]
    pack_ref[spots[1]:spots[1] + mid, :] = acc_e[...]
    pack_ref[spots[2]:spots[2] + 3 * mid, :3 * mid] = acc_s[...]


def layout(mid, heads):
    first = -(-9 * heads // 8) * 8
    return first, first + mid, first + 2 * mid, first + 5 * mid


def piece_rows(s, orders, sizes, total):
    rows, out = total // len(orders), []
    for axis in orders[s]:
        rows //= sizes[axis]
        out.append(rows)
    return out


def sum_kernel(sizes, orders, pack_ref, stat_ref, out_ref, total_ref, *scratch):
    subs, depth = len(orders), len(AXES)
    send, full = scratch[0], scratch[1]
    recvs = [scratch[2 + s * depth:2 + (s + 1) * depth] for s in range(subs)]
    stat_send = scratch[2 + subs * depth]
    stat_recv = scratch[3 + subs * depth:3 + subs * depth + depth]
    ssem, rsem = scratch[-2:]
    total = pack_ref.shape[0]
    share = total // subs
    me = {axis: lax.axis_index(axis) for axis in AXES}
    peers = lambda axis: range(1, sizes[axis])
    mesh_id = pl.DeviceIdType.MESH

    barrier = pltpu.get_barrier_semaphore()
    for axis in AXES:
        for d in peers(axis):
            pl.semaphore_signal(
                barrier, inc=1, device_id={axis: lax.rem(me[axis] + d, sizes[axis])},
                device_id_type=mesh_id,
            )
    pl.semaphore_wait(barrier, sum(sizes[axis] - 1 for axis in AXES))

    used = [0]

    def push(src, dst, axis, d):
        n = used[0]
        used[0] += 1
        copy = pltpu.make_async_remote_copy(
            src_ref=src, dst_ref=dst, send_sem=ssem.at[n], recv_sem=rsem.at[n],
            device_id={axis: lax.rem(me[axis] + d, sizes[axis])}, device_id_type=mesh_id,
        )
        copy.start()
        return copy

    send[...] = pack_ref[...].astype(BF16)
    base = [s * share for s in range(subs)]
    held = [None] * subs
    stat = stat_ref[...]
    for k in range(depth):
        copies = []
        for s in range(subs):
            axis = orders[s][k]
            rows = piece_rows(s, orders, sizes, total)[k]
            for d in peers(axis):
                to = lax.rem(me[axis] + d, sizes[axis])
                src = send.at[pl.ds(pl.multiple_of(base[s] + to * rows, 16), rows)]
                copies.append(push(src, recvs[s][k].at[d - 1], axis, d))
        stat_send[k] = stat
        for d in peers(AXES[k]):
            copies.append(push(stat_send.at[k], stat_recv[k].at[d - 1], AXES[k], d))
        for copy in copies:
            copy.wait()
        for d in peers(AXES[k]):
            stat = stat + stat_recv[k][d - 1]
        for s in range(subs):
            axis = orders[s][k]
            rows = piece_rows(s, orders, sizes, total)[k]
            mine = me[axis] * rows
            if k == 0:
                got = pack_ref[pl.ds(pl.multiple_of(base[s] + mine, 16), rows), :]
            else:
                out_at = pl.ds(pl.multiple_of(base[s] + mine, 16), rows)
                got = out_ref[out_at, :]
            for d in peers(axis):
                got = got + recvs[s][k][d - 1].astype(F32)
            base[s] = pl.multiple_of(base[s] + mine, 16)
            where = pl.ds(base[s], rows)
            if k < depth - 1:
                out_ref[where, :] = got
                send[where, :] = got.astype(BF16)
            else:
                full[where, :] = got.astype(BF16)
    total_ref[...] = stat
    for k in range(depth - 1, -1, -1):
        copies = []
        for s in range(subs):
            axis = orders[s][k]
            rows = piece_rows(s, orders, sizes, total)[k]
            where = pl.ds(base[s], rows)
            for d in peers(axis):
                copies.append(push(full.at[where], full.at[where], axis, d))
            base[s] = pl.multiple_of(base[s] - me[axis] * rows, 16)
        for copy in copies:
            copy.wait()
    out_ref[...] = full[...].astype(F32)


def sum_devices(pack, stat):
    sizes = {axis: lax.axis_size(axis) for axis in AXES}
    orders = [AXES[s:] + AXES[:s] for s in range(len(AXES))]
    total, chans = pack.shape
    scratch = [pltpu.VMEM((total, chans), BF16), pltpu.VMEM((total, chans), BF16)]
    copies = 0
    for s in range(len(orders)):
        for axis, rows in zip(orders[s], piece_rows(s, orders, sizes, total)):
            scratch.append(pltpu.VMEM((max(sizes[axis] - 1, 1), rows, chans), BF16))
            copies += 2 * (sizes[axis] - 1)
    scratch.append(pltpu.VMEM((len(AXES),) + stat.shape, F32))
    for axis in AXES:
        scratch.append(pltpu.VMEM((max(sizes[axis] - 1, 1),) + stat.shape, F32))
        copies += sizes[axis] - 1
    scratch += [pltpu.SemaphoreType.DMA((copies,)), pltpu.SemaphoreType.DMA((copies,))]
    return pl.pallas_call(
        functools.partial(sum_kernel, sizes, orders),
        out_shape=(
            jax.ShapeDtypeStruct(pack.shape, F32), jax.ShapeDtypeStruct(stat.shape, F32)
        ),
        in_specs=[pl.BlockSpec(memory_space=pltpu.VMEM)] * 2,
        out_specs=[pl.BlockSpec(memory_space=pltpu.VMEM)] * 2,
        scratch_shapes=scratch,
        compiler_params=pltpu.CompilerParams(
            collective_id=0, has_side_effects=True, vmem_limit_bytes=16 * 1024 * 1024
        ),
        name="sum_devices",
    )(pack, stat)


def per_device(
    inputs, reduce_weight, spatial_weight, expand_weight, class_weight, anchor_labels, anchor_mask
):
    tiles, chans, rows, cols = inputs.shape
    assert tiles == 1
    mid = reduce_weight.shape[0]
    heads = class_weight.shape[2]
    outs = -(-heads // 16) * 16
    sizes = {axis: lax.axis_size(axis) for axis in ("row", "col")}

    code = jnp.where(anchor_mask[0] > 0, anchor_labels[0], 64).astype(BF16)
    code = jnp.concatenate([
        code, jnp.ones((1, rows, cols), BF16), jnp.zeros((16 - A - 1, rows, cols), BF16)
    ], axis=0).transpose(1, 0, 2)
    x = inputs[0].transpose(1, 0, 2)

    spread = np.zeros((outs, 16), np.float32)
    spread[np.arange(heads), np.arange(heads) // K] = 1.0
    spread[np.arange(heads), A] = -1.0 - np.arange(heads) % K
    spread[heads:, A] = 64.0
    spread = jnp.asarray(spread, BF16)

    flip = lambda w: w[::-1, ::-1].transpose(0, 3, 1, 2)
    wide = jnp.pad(class_weight, ((0, 0), (0, 0), (0, outs - heads), (0, 0)))
    ws = spatial_weight.transpose(0, 2, 1, 3).reshape(3, mid, 3 * mid)
    wsb = flip(spatial_weight).reshape(3, mid, 3 * mid)
    wc = wide.transpose(0, 2, 1, 3).reshape(3, outs, 3 * chans)
    wcb = flip(wide).reshape(3, chans, 3 * outs)

    unit = 16 * len(AXES) * int(np.prod([lax.axis_size(axis) for axis in AXES]))
    packed = -(-layout(mid, heads)[3] // unit) * unit
    depths = (mid, chans, outs, mid)

    sums = pl.pallas_call(
        functools.partial(step_kernel, sizes, heads),
        out_shape=(
            jax.ShapeDtypeStruct((packed, chans), F32),
            jax.ShapeDtypeStruct((8, 128), F32),
        ),
        in_specs=[pl.BlockSpec(memory_space=pltpu.VMEM)] * 10,
        out_specs=[pl.BlockSpec(memory_space=pltpu.VMEM)] * 2,
        scratch_shapes=[
            pltpu.VMEM((rows + 2, 3 * mid, cols), BF16),
            pltpu.VMEM((rows, mid, cols), BF16),
            pltpu.VMEM((rows + 2, 3 * chans, cols), BF16),
            pltpu.VMEM((rows + 2, 3 * outs, cols), BF16),
            pltpu.VMEM((rows + 2, outs, cols), BF16),
            pltpu.VMEM((rows + 2, 3 * mid, cols), BF16),
            pltpu.VMEM((rows + 2, mid, cols), BF16),
            pltpu.VMEM((3 * outs, 3 * chans), F32),
            pltpu.VMEM((3 * mid, 3 * mid), F32),
            pltpu.VMEM((mid, chans), F32),
            pltpu.VMEM((mid, chans), F32),
            [pltpu.VMEM((depth, cols), BF16) for depth in depths],
            [pltpu.VMEM((2, depth, cols), BF16) for depth in depths],
            pltpu.SemaphoreType.DMA((16,)),
            pltpu.SemaphoreType.DMA((16,)),
        ],
        compiler_params=pltpu.CompilerParams(
            collective_id=1, has_side_effects=True, vmem_limit_bytes=56 * 1024 * 1024
        ),
        name="tile_step",
    )(x, code, spread, reduce_weight, ws, wsb, expand_weight, expand_weight.T, wc, wcb)
    return finish(sums, mid, heads)


def finish(sums, mid, heads):
    pack, stat = sum_devices(*sums)
    chans = pack.shape[1]
    spots = layout(mid, heads)
    count = jnp.sum(stat[1])
    scale = 1.0 / count
    spatial = pack[spots[2]:spots[3], :3 * mid].reshape(3, mid, 3, mid).transpose(0, 2, 1, 3)
    return (
        jnp.sum(stat[0]) / count,
        pack[spots[0]:spots[1]] * scale,
        spatial * scale,
        pack[spots[1]:spots[2]].T * scale,
        pack[:9 * heads].reshape(3, 3, heads, chans) * scale,
    )


def solution(mesh):
    tiled = P("dp", None, "row", "col")
    return jax.shard_map(
        per_device,
        mesh=mesh,
        in_specs=(tiled, P(), P(), P(), P(), tiled, tiled),
        out_specs=(P(), P(), P(), P(), P()),
        check_vma=False,
    )
```

time: 125 us -> 123 us (0.984)
  Pallas kernels: 106 us -> 101 us
  local copies, waits for them, and re-layouts: 12 us -> 15.3 us
    pallas_call x2 -> x1, Pallas kernels: 70.5 us -> 66.8 us  [per_device(): pl.pallas_call(functools.partial(step_kernel, sizes, heads), out_shape=(j...]
    unnamed x15 -> x9, local copies, waits for them, and re-layouts: 5.45 us -> 8.09 us
    reshape x4, local copies, waits for them, and re-layouts: 2.33 us -> 3.59 us  [the longest x1 1.16 us: per_device(): wcb = flip(wide).reshape(3, chans, 3 * outs)]
where the time goes in v1:
time: 123 us
  Pallas kernels  101 us (82%)
  local copies, waits for them, and re-layouts  15.3 us (12%)
  between operations  3.86 us (3%)
  other arithmetic  3.29 us (3%)
    pallas_call x1, Pallas kernels, per_device(): pl.pallas_call(functools.partial(step_kernel, sizes, heads), out_shape=(j...  66.8 us
    pallas_call x1, Pallas kernels, sum_devices(): pl.pallas_call(functools.partial(sum_kernel, sizes, orders), out_shape=(j...  33.8 us
    unnamed x9, local copies, waits for them, and re-layouts  8.09 us

profile of v1, /device:TPU:0, one launch (start us, length us, event | category | flops | bytes accessed | tf_op | source)
XLA Modules:
  0.0 123.0 jit_solution(6105559621176676167)
XLA Ops:
  0.6 0.0 copy-start.2
  0.6 0.1 pad.6.clone
  0.7 0.1 pad.7.clone
  0.8 1.5 %copy.29.we_ref = bf16[256,64]{1,0:T(8,128)(2,1)} copy(bf16[256,64]{0,1:T(8,128)(2,1)} %param.11) | data formatting | bytes 65536 | tf_op args[3]
  2.3 1.2 fusion.1
  3.5 0.8 maximum_bitcast_fusion.code_ref
  4.3 1.0 copy.25
  5.3 0.8 copy.27.ws_ref
  6.1 0.9 rev.6
  7.0 0.8 copy.28.wsb_ref
  7.8 0.0 copy-done.2
  7.8 0.1 fusion.2
  7.9 1.2 copy.30.wcb_ref
  9.1 0.9 copy.32
  10.0 3.7 %copy.44 = bf16[1,256,32,128]{3,1,2,0:T(8,128)(2,1)} copy(bf16[1,256,32,128]{3,2,1,0:T(8,128)(2,1)} %param.8) | data formatting | bytes 4194304 | tf_op args[0]
  13.7 66.8 %tile_step.1 = (f32[1536,256]{1,0:T(8,128)}, f32[8,128]{1,0:T(8,128)}) custom-call(bf16[32,256,128]{2,1,0:T(8,128)(2,1)} %bitcast.26, bf16[32,16,128]{2,1,0:T(8,128)(2,1)} %maximum_bitcast_fusion.code_ref, bf16[144,16]{1,0:T(8,128)(2,1)} %constant.16.clone.spread_ref, bf16[64,256]{1,0:T(8,128)(2,1)} %wr_ref.1, bf16[3,64,192]{2,1,0:T(8,128)(2,1)} %copy.27.ws_ref, ...), custom_call_target="tpu_custom_call" | custom-call | tf_op jit(solution)/shard_map/tile_step/pallas_call | solution.py:435
  80.5 0.0 copy-start
  80.5 1.4 %copy-done = f32[1536,256]{1,0:T(8,128)S(1)} copy-done((f32[1536,256]{1,0:T(8,128)S(1)}, f32[1536,256]{1,0:T(8,128)}, u32[]{:S(2)}) %copy-start) | copy-done | bytes 1572888
  81.9 0.0 copy-start.1
  81.9 0.7 copy-done.1
  82.6 33.8 %sum_devices.1 = (f32[1536,256]{1,0:T(8,128)S(1)}, f32[8,128]{1,0:T(8,128)S(1)}) custom-call(f32[1536,256]{1,0:T(8,128)S(1)} %copy-done, f32[8,128]{1,0:T(8,128)S(1)} %copy-done.1), custom_call_target="tpu_custom_call" | custom-call | tf_op jit(solution)/shard_map/sum_devices/pallas_call | solution.py:387
  116.4 0.6 slice_reduce_fusion
  119.1 0.7 multiply_bitcast_fusion
  119.7 0.1 slice_multiply_fusion
  119.8 1.2 mul.44
  121.0 0.2 mul.38
  121.2 0.7 copy.31
  (3 shorter events, 0.1 us)
Async XLA Ops:
  0.6 7.1 %copy-start.2 = (bf16[3,3,135,256]{3,2,1,0:T(8,128)(2,1)S(1)}, bf16[3,3,135,256]{3,2,1,0:T(8,128)(2,1)}, u32[]{:S(2)}) copy-start(bf16[3,3,135,256]{3,2,1,0:T(8,128)(2,1)} %param.12) | copy-start | bytes 1866244
  80.5 1.4 %copy-start = (f32[1536,256]{1,0:T(8,128)S(1)}, f32[1536,256]{1,0:T(8,128)}, u32[]{:S(2)}) copy-start(f32[1536,256]{1,0:T(8,128)} %get-tuple-element.9.pack_ref) | copy-start | bytes 4718596
  81.9 0.7 copy-start.1

commit v2 on v1

--- a/solution.py
+++ b/solution.py
@@ -29,14 +29,14 @@
 
 def step_kernel(
     sizes, heads,
-    x_ref, code_ref, spread_ref, wr_ref, ws_ref, wsb_ref, we_ref, wet_ref, wc_ref, wcb_ref,
+    x_ref, label_ref, mask_ref, spread_ref, wr_ref, spatial_ref, we_ref, class_ref,
     pack_ref, stat_ref,
     first, second, block, dlog, dzero, dsec, dsec_zero, acc_c, acc_s, acc_e, acc_r,
-    strips, got, ssem, rsem,
+    code_ref, ws_ref, wsb_ref, wet_ref, wc_ref, wcb_ref, strips, got, ssem, rsem,
 ):
     rows, chans, cols = x_ref.shape
     mid = wr_ref.shape[0]
-    outs = wc_ref.shape[1]
+    outs = wc_ref.shape[2]
     me = {axis: lax.axis_index(axis) for axis in ("row", "col")}
     mesh_id = pl.DeviceIdType.MESH
     sides = [(axis, step) for axis in ("row", "col") for step in (1, -1)]
@@ -110,18 +110,21 @@
         )
         return down, up
 
+    def publish(n, field, depth, at, value):
+        lane = lax.broadcasted_iota(jnp.int32, (depth, cols), 1) // 2
+        for k in range(value.shape[1] // cols):
+            row = value[:, k * cols:(k + 1) * cols]
+            i = at + k
+            field[i, depth:2 * depth, :] = row
+            field[i, :depth, :] = pltpu.roll(row, 1, 1)
+            field[i, 2 * depth:, :] = pltpu.roll(row, cols - 1, 1)
+            strips[n][...] = jnp.where(lane == i, pltpu.roll(row, 2 * i + 1, 1), strips[n][...])
+
     def send_strip(n, field, depth, held):
-        lane = lax.broadcasted_iota(jnp.int32, (depth, cols), 1)
-
-        def gather(i, strip):
-            row = field[i, depth:2 * depth, :]
-            return jnp.where(lane // 2 == i, pltpu.roll(row, 2 * i + 1, 1), strip)
-
-        strip = lax.fori_loop(1, rows + 1, gather, jnp.zeros((depth, cols), BF16))
         for wait in held:
             wait()
-        strip = gather(rows + 1, gather(0, strip))
-        strips[n][...] = strip
+        for i in (0, rows + 1):
+            publish(n, field, depth, i, field[i, depth:2 * depth, :])
         right = push(4 * n + 2, strips[n], got[n].at[0], "col", 1)
         left = push(4 * n + 3, strips[n], got[n].at[1], "col", -1)
         return right, left
@@ -131,26 +134,28 @@
             wait()
         lane = lax.broadcasted_iota(jnp.int32, (depth, cols), 1)
         before, after = got[n][0], got[n][1]
-
-        def fill(i, c):
-            row = field[i, depth:2 * depth, :]
+        for i in range(rows + 2):
             field[i, :depth, :] = jnp.where(
-                lane == 0, pltpu.roll(before, cols - 2 * i, 1), pltpu.roll(row, 1, 1)
+                lane == 0, pltpu.roll(before, (cols - 2 * i) % cols, 1), field[i, :depth, :]
             )
             field[i, 2 * depth:, :] = jnp.where(
-                lane == cols - 1, pltpu.roll(after, cols - 2 - 2 * i, 1),
-                pltpu.roll(row, cols - 1, 1),
+                lane == cols - 1, pltpu.roll(after, (cols - 2 - 2 * i) % cols, 1),
+                field[i, 2 * depth:, :],
             )
-            return c
-
-        loop(rows + 2, fill)
 
     def conv(weight, field, at):
-        return sum(dot(weight[dy], cat(field, at + dy, GROUP)) for dy in range(3))
+        return sum(dot(weight(dy), cat(field, at + dy, GROUP)) for dy in range(3))
+
+    def sweep(body, between, init=0):
+        groups = rows // GROUP
+        carry = loop(2, lambda j, c: body(j * (groups - 1), c), init)
+        held = between()
+        return held, loop(groups - 2, lambda j, c: body(j + 1, c), carry)
 
     fields = [(first, mid), (block, chans), (dlog, outs), (dsec, mid)]
     for n, (field, depth) in enumerate(fields):
         clear_edges(n, field, depth)
+        strips[n][...] = jnp.zeros((depth, cols), BF16)
     for ref in (dzero, dsec_zero):
         ref[0] = jnp.zeros(ref.shape[1:], BF16)
         ref[rows + 1] = jnp.zeros(ref.shape[1:], BF16)
@@ -161,29 +166,52 @@
 
     def make_first(i, c):
         z = dot(wr_ref[...], cat(x_ref, i * GROUP, GROUP))
-        spread_rows(first, i * GROUP + 1, jnp.maximum(z, 0.0).astype(BF16), mid, 2 * mid)
+        publish(0, first, mid, i * GROUP + 1, jnp.maximum(z, 0.0).astype(BF16))
         return c
 
-    loop(rows // GROUP, make_first)
-    held = send_rows(0, first, mid)
+    held, _ = sweep(make_first, lambda: send_rows(0, first, mid))
+    for dy in range(3):
+        for dx in range(3):
+            ws_ref[dy, :, dx * mid:(dx + 1) * mid] = spatial_ref[dy, dx]
+            wc_ref[dy, dx, :heads, :] = class_ref[dy, dx]
+            wc_ref[dy, dx, heads:, :] = jnp.zeros((outs - heads, chans), BF16)
+    for h in range(rows):
+        code = jnp.where(mask_ref[:, h, :] > 0, label_ref[:, h, :], 64)
+        code_ref[h, :A, :] = code.astype(F32).astype(BF16)
+        code_ref[h, A:, :] = jnp.ones((16 - A, cols), BF16)
     held = send_strip(0, first, mid, held)
+
+    def turned(parts):
+        size = parts[0].shape[1]
+        eye = jnp.where(
+            lax.broadcasted_iota(jnp.int32, (size, size), 0)
+            == lax.broadcasted_iota(jnp.int32, (size, size), 1), 1.0, 0.0,
+        ).astype(BF16)
+        return dot_t(eye, jnp.concatenate(parts, axis=0)).astype(BF16)
+
+    wet_ref[...] = turned([we_ref[...]])
+    for dy in range(3):
+        wsb_ref[dy] = turned([spatial_ref[2 - dy, 2 - dx] for dx in range(3)])
+        wcb_ref[dy] = turned([wc_ref[2 - dy, 2 - dx] for dx in range(3)])
     widen(0, first, mid, held)
 
     def make_block(i, c):
-        s = jnp.maximum(conv(ws_ref, first, i * GROUP), 0.0).astype(BF16)
+        s = jnp.maximum(conv(lambda dy: ws_ref[dy], first, i * GROUP), 0.0).astype(BF16)
         spread_rows(second, i * GROUP, s)
         b = jnp.maximum(cat(x_ref, i * GROUP, GROUP).astype(F32) + dot(we_ref[...], s), 0.0)
-        spread_rows(block, i * GROUP + 1, b.astype(BF16), chans, 2 * chans)
+        publish(1, block, chans, i * GROUP + 1, b.astype(BF16))
         return c
 
-    loop(rows // GROUP, make_block)
-    held = send_rows(1, block, chans)
+    held, _ = sweep(make_block, lambda: send_rows(1, block, chans))
     held = send_strip(1, block, chans, held)
     widen(1, block, chans, held)
 
+    def class_rows(dy):
+        return jnp.concatenate([wc_ref[dy, dx] for dx in range(3)], axis=1)
+
     def make_dlog(i, carry):
         total, count = carry
-        z = conv(wc_ref, block, i * GROUP)
+        z = conv(class_rows, block, i * GROUP)
         code = cat(code_ref, i * GROUP, GROUP)
         gap = dot(spread_ref[...], code)
         target = gap == 0.0
@@ -197,7 +225,7 @@
         total = total + jnp.sum(scaled * soft, axis=0, keepdims=True)
         slope = scaled * ((2.0 * LN2 - 2.0 * LN2 * prob) * soft + prob)
         d = jnp.where(target, -slope, slope).astype(BF16)
-        spread_rows(dlog, i * GROUP + 1, d, outs, 2 * outs)
+        publish(2, dlog, outs, i * GROUP + 1, d)
         spread_rows(dzero, i * GROUP + 1, d)
         codes = code.astype(F32)
         row = lax.broadcasted_iota(jnp.int32, codes.shape, 0)
@@ -206,12 +234,11 @@
         return total, count
 
     zero = jnp.zeros((1, GROUP * cols), F32)
-    total, count = loop(rows // GROUP, make_dlog, (zero, zero))
+    held, (total, count) = sweep(make_dlog, lambda: send_rows(2, dlog, outs), (zero, zero))
     fold = lambda v: sum(v[:, k * 128:(k + 1) * 128] for k in range(v.shape[1] // 128))
     stat_ref[0:1, :] = fold(total) * LN2
     stat_ref[1:2, :] = fold(count)
     stat_ref[2:, :] = jnp.zeros((6, 128), F32)
-    held = send_rows(2, dlog, outs)
 
     def weight_sum(acc, grad, field):
         depth = grad.shape[1]
@@ -231,25 +258,24 @@
     widen(2, dlog, outs, held)
 
     def make_dsec(i, c):
-        g = conv(wcb_ref, dlog, i * GROUP)
+        g = conv(lambda dy: wcb_ref[dy], dlog, i * GROUP)
         b = cat(block, i * GROUP + 1, GROUP, chans, 2 * chans).astype(F32)
         ds = jnp.where(b > 0.0, g, 0.0).astype(BF16)
         s = cat(second, i * GROUP, GROUP)
         acc_e[...] += dot_t(s, ds)
         h = dot(wet_ref[...], ds)
         d = jnp.where(s.astype(F32) > 0.0, h, 0.0).astype(BF16)
-        spread_rows(dsec, i * GROUP + 1, d, mid, 2 * mid)
+        publish(3, dsec, mid, i * GROUP + 1, d)
         spread_rows(dsec_zero, i * GROUP + 1, d)
         return c
 
-    loop(rows // GROUP, make_dsec)
-    held = send_rows(3, dsec, mid)
+    held, _ = sweep(make_dsec, lambda: send_rows(3, dsec, mid))
     weight_sum(acc_s, dsec_zero, first)
     held = send_strip(3, dsec, mid, held)
     widen(3, dsec, mid, held)
 
     def make_dfirst(i, c):
-        g = conv(wsb_ref, dsec, i * GROUP)
+        g = conv(lambda dy: wsb_ref[dy], dsec, i * GROUP)
         f = cat(first, i * GROUP + 1, GROUP, mid, 2 * mid).astype(F32)
         df = jnp.where(f > 0.0, g, 0.0).astype(BF16)
         acc_r[...] += dot_t(df, cat(x_ref, i * GROUP, GROUP))
@@ -409,10 +435,6 @@
     outs = -(-heads // 16) * 16
     sizes = {axis: lax.axis_size(axis) for axis in ("row", "col")}
 
-    code = jnp.where(anchor_mask[0] > 0, anchor_labels[0], 64).astype(BF16)
-    code = jnp.concatenate([
-        code, jnp.ones((1, rows, cols), BF16), jnp.zeros((16 - A - 1, rows, cols), BF16)
-    ], axis=0).transpose(1, 0, 2)
     x = inputs[0].transpose(1, 0, 2)
 
     spread = np.zeros((outs, 16), np.float32)
@@ -420,13 +442,6 @@
     spread[np.arange(heads), A] = -1.0 - np.arange(heads) % K
     spread[heads:, A] = 64.0
     spread = jnp.asarray(spread, BF16)
-
-    flip = lambda w: w[::-1, ::-1].transpose(0, 3, 1, 2)
-    wide = jnp.pad(class_weight, ((0, 0), (0, 0), (0, outs - heads), (0, 0)))
-    ws = spatial_weight.transpose(0, 2, 1, 3).reshape(3, mid, 3 * mid)
-    wsb = flip(spatial_weight).reshape(3, mid, 3 * mid)
-    wc = wide.transpose(0, 2, 1, 3).reshape(3, outs, 3 * chans)
-    wcb = flip(wide).reshape(3, chans, 3 * outs)
 
     unit = 16 * len(AXES) * int(np.prod([lax.axis_size(axis) for axis in AXES]))
     packed = -(-layout(mid, heads)[3] // unit) * unit
@@ -438,7 +453,7 @@
             jax.ShapeDtypeStruct((packed, chans), F32),
             jax.ShapeDtypeStruct((8, 128), F32),
         ),
-        in_specs=[pl.BlockSpec(memory_space=pltpu.VMEM)] * 10,
+        in_specs=[pl.BlockSpec(memory_space=pltpu.VMEM)] * 8,
         out_specs=[pl.BlockSpec(memory_space=pltpu.VMEM)] * 2,
         scratch_shapes=[
             pltpu.VMEM((rows + 2, 3 * mid, cols), BF16),
@@ -452,6 +467,12 @@
             pltpu.VMEM((3 * mid, 3 * mid), F32),
             pltpu.VMEM((mid, chans), F32),
             pltpu.VMEM((mid, chans), F32),
+            pltpu.VMEM((rows, 16, cols), BF16),
+            pltpu.VMEM((3, mid, 3 * mid), BF16),
+            pltpu.VMEM((3, mid, 3 * mid), BF16),
+            pltpu.VMEM((mid, chans), BF16),
+            pltpu.VMEM((3, 3, outs, chans), BF16),
+            pltpu.VMEM((3, chans, 3 * outs), BF16),
             [pltpu.VMEM((depth, cols), BF16) for depth in depths],
             [pltpu.VMEM((2, depth, cols), BF16) for depth in depths],
             pltpu.SemaphoreType.DMA((16,)),
@@ -461,7 +482,10 @@
             collective_id=1, has_side_effects=True, vmem_limit_bytes=56 * 1024 * 1024
         ),
         name="tile_step",
-    )(x, code, spread, reduce_weight, ws, wsb, expand_weight, expand_weight.T, wc, wcb)
+    )(
+        x, anchor_labels[0], anchor_mask[0], spread, reduce_weight, spatial_weight,
+        expand_weight, class_weight,
+    )
     return finish(sums, mid, heads)
 
 

time: 123 us -> 97.9 us (0.80)
  Pallas kernels: 101 us -> 83 us
  local copies, waits for them, and re-layouts: 15.3 us -> 9.41 us
  other arithmetic: 3.29 us -> 1.36 us
    pallas_call x1, Pallas kernels: 66.8 us -> 50 us  [per_device(): pl.pallas_call(functools.partial(step_kernel, sizes, heads), out_shape=(j...]
    reshape x4 -> x0, local copies, waits for them, and re-layouts: 3.59 us -> none  [the longest x1 1.16 us: per_device(): wcb = flip(wide).reshape(3, chans, 3 * outs)]
    unnamed x9 -> x7, local copies, waits for them, and re-layouts: 8.09 us -> 8.06 us
where the time goes in v2:
time: 97.9 us; the launch traced here: 97.6 us
  Pallas kernels  83 us (85%)
  local copies, waits for them, and re-layouts  9.41 us (10%)
  between operations  3.83 us (4%)
  other arithmetic  1.36 us (1%)
    pallas_call x1, Pallas kernels, per_device(): pl.pallas_call(functools.partial(step_kernel, sizes, heads), out_shape=(j...  50 us
    pallas_call x1, Pallas kernels, sum_devices(): pl.pallas_call(functools.partial(sum_kernel, sizes, orders), out_shape=(j...  33 us
    unnamed x7, local copies, waits for them, and re-layouts  8.06 us

profile of v2, /device:TPU:0, one launch (start us, length us, event | category | flops | bytes accessed | tf_op | source)
XLA Modules:
  0.0 97.6 jit_solution(7524435169078649714)
XLA Ops:
  0.6 1.5 %copy.17.we_ref = bf16[256,64]{1,0:T(8,128)(2,1)} copy(bf16[256,64]{0,1:T(8,128)(2,1)} %param.11) | data formatting | bytes 65536 | tf_op args[3]
  2.1 3.7 %copy.20 = bf16[1,256,32,128]{3,1,2,0:T(8,128)(2,1)} copy(bf16[1,256,32,128]{3,2,1,0:T(8,128)(2,1)} %param.8) | data formatting | bytes 4194304 | tf_op args[0]
  5.9 50.0 %tile_step.1 = (f32[1536,256]{1,0:T(8,128)}, f32[8,128]{1,0:T(8,128)}) custom-call(bf16[32,256,128]{2,1,0:T(8,128)(2,1)} %bitcast.10, s32[9,32,128]{2,1,0:T(8,128)} %bitcast.12, s32[9,32,128]{2,1,0:T(8,128)} %bitcast.13, bf16[144,16]{1,0:T(8,128)(2,1)} %constant.6.clone.spread_ref, bf16[64,256]{1,0:T(8,128)(2,1)} %wr_ref.1, ...), custom_call_target="tpu_custom_call" | custom-call | tf_op jit(solution)/shard_map/tile_step/pallas_call | solution.py:450
  55.9 0.0 copy-start
  55.9 1.4 %copy-done = f32[1536,256]{1,0:T(8,128)S(1)} copy-done((f32[1536,256]{1,0:T(8,128)S(1)}, f32[1536,256]{1,0:T(8,128)}, u32[]{:S(2)}) %copy-start) | copy-done | bytes 1572888
  57.3 0.0 copy-start.1
  57.3 0.7 copy-done.1
  58.0 33.0 %sum_devices.1 = (f32[1536,256]{1,0:T(8,128)S(1)}, f32[8,128]{1,0:T(8,128)S(1)}) custom-call(f32[1536,256]{1,0:T(8,128)S(1)} %copy-done, f32[8,128]{1,0:T(8,128)S(1)} %copy-done.1), custom_call_target="tpu_custom_call" | custom-call | tf_op jit(solution)/shard_map/sum_devices/pallas_call | solution.py:413
  91.0 0.6 slice_reduce_fusion
  93.6 0.7 multiply_bitcast_fusion
  94.3 0.1 slice_multiply_fusion
  94.4 1.2 %mul.44 = f32[3,3,135,256]{3,2,1,0:T(8,128)} reshape(f32[1215,256]{1,0:T(8,128)S(1)} %slice_multiply_fusion) | data formatting | bytes 2488320 | tf_op jit(solution)/shard_map/mul | solution.py:504
  95.6 0.2 mul.38
  95.7 0.7 copy.18
  (1 shorter events, 0.0 us)
Async XLA Ops:
  55.9 1.4 %copy-start = (f32[1536,256]{1,0:T(8,128)S(1)}, f32[1536,256]{1,0:T(8,128)}, u32[]{:S(2)}) copy-start(f32[1536,256]{1,0:T(8,128)} %get-tuple-element.9.pack_ref) | copy-start | bytes 4718596
  57.3 0.7 copy-start.1

commit v3 on v2

v3 whole, which is shorter than its diff:
```python
import functools

import jax
import jax.numpy as jnp
import numpy as np
from jax import lax
from jax.experimental import pallas as pl
from jax.experimental.pallas import tpu as pltpu
from jax.sharding import PartitionSpec as P

A = 9
K = 15
GROUP = 4
WIDE = 8
LOG2E = 1.4426950408889634
LN2 = 0.6931471805599453
F32 = jnp.float32
BF16 = jnp.bfloat16
AXES = ("dp", "row", "col")


def dot(a, b):
    return jnp.dot(a, b, preferred_element_type=F32)


def dot_t(a, b):
    return lax.dot_general(a, b, (((1,), (1,)), ((), ())), preferred_element_type=F32)


def step_kernel(
    sizes, orders, heads,
    x_ref, label_ref, mask_ref, spread_ref, wr_ref, spatial_ref, we_ref, class_ref,
    loss_ref, grad_reduce_ref, grad_spatial_ref, grad_expand_ref, grad_class_ref,
    first, second, block, dlog, dzero, dsec, dsec_zero, acc_c, acc_s, acc_e, acc_r,
    code_ref, ws_ref, wsb_ref, wet_ref, wc_ref, wcb_ref, strips, got,
    stat, stat_slots, big_send, big_work, big_full, big_slots, mid_refs, tail_refs, ssem, rsem,
):
    rows, chans, cols = x_ref.shape
    mid = wr_ref.shape[0]
    outs = wc_ref.shape[2]
    me = {axis: lax.axis_index(axis) for axis in AXES}
    mesh_id = pl.DeviceIdType.MESH
    peers = lambda axis: range(1, sizes[axis])
    used = [0]

    def exists(axis, step):
        return me[axis] < sizes[axis] - 1 if step > 0 else me[axis] > 0

    barrier = pltpu.get_barrier_semaphore()
    for axis in AXES:
        for d in peers(axis):
            pl.semaphore_signal(
                barrier, inc=1, device_id={axis: lax.rem(me[axis] + d, sizes[axis])},
                device_id_type=mesh_id,
            )

    def remote(src, dst, axis, to):
        n = used[0]
        used[0] += 1
        return pltpu.make_async_remote_copy(
            src_ref=src, dst_ref=dst, send_sem=ssem.at[n], recv_sem=rsem.at[n],
            device_id={axis: to}, device_id_type=mesh_id,
        )

    def push(src, dst, axis, step):
        copy = remote(src, dst, axis, me[axis] + step)

        @pl.when(exists(axis, step))
        def _():
            copy.start()

        def finish():
            @pl.when(exists(axis, step))
            def _():
                copy.wait_send()

            @pl.when(exists(axis, -step))
            def _():
                copy.wait_recv()

        return finish

    def post(copies, src, dst, axis, d):
        copy = remote(src, dst, axis, lax.rem(me[axis] + d, sizes[axis]))
        copy.start()
        copies.append(copy)

    def settle(copies):
        for copy in copies:
            copy.wait()
        copies.clear()

    def total_of(slots):
        return sum(slots[j].astype(F32) for j in range(slots.shape[0]))

    def reduce_stats():
        copies = []
        value = stat[...]
        for k, axis in enumerate(AXES):
            slot = stat_slots[k].at[me[axis]]
            slot[...] = value
            for d in peers(axis):
                post(copies, slot, slot, axis, d)
            yield
            settle(copies)
            value = total_of(stat_slots[k])
        stat[...] = value

    def reduce_big(orders):
        share = big_send.shape[0] // len(orders)
        base = [s * share for s in range(len(orders))]
        copies = []
        part = lambda s, rows: pl.ds(pl.multiple_of(base[s], 16), rows)
        for k in range(len(AXES)):
            for s, order in enumerate(orders):
                axis, piece = order[k], big_slots[s][k].shape[1]
                for d in peers(axis):
                    to = lax.rem(me[axis] + d, sizes[axis])
                    src = big_send.at[pl.ds(pl.multiple_of(base[s] + to * piece, 16), piece)]
                    post(copies, src, big_slots[s][k].at[d - 1], axis, d)
            yield
            settle(copies)
            for s, order in enumerate(orders):
                axis, piece = order[k], big_slots[s][k].shape[1]
                base[s] = base[s] + me[axis] * piece
                at = part(s, piece)
                value = (big_work if k else big_send)[at, :].astype(F32)
                for d in peers(axis):
                    value = value + big_slots[s][k][d - 1].astype(F32)
                if k < len(AXES) - 1:
                    big_work[at, :] = value
                    big_send[at, :] = value.astype(BF16)
                else:
                    big_full[at, :] = value.astype(BF16)
        for k in reversed(range(len(AXES))):
            for s, order in enumerate(orders):
                axis, piece = order[k], big_slots[s][k].shape[1]
                at = part(s, piece)
                for d in peers(axis):
                    post(copies, big_full.at[at], big_full.at[at], axis, d)
                base[s] = base[s] - me[axis] * piece
            yield
            settle(copies)

    def reduce_small(refs):
        send, full, across, tile_slots, row_slots = refs
        piece = across.shape[1]
        copies = []
        mine = pl.ds(pl.multiple_of(me["col"] * piece, 16), piece)
        across[me["col"]] = send[mine, :]
        for d in peers("col"):
            to = lax.rem(me["col"] + d, sizes["col"])
            src = send.at[pl.ds(pl.multiple_of(to * piece, 16), piece)]
            post(copies, src, across.at[me["col"]], "col", d)
        yield
        settle(copies)
        value = total_of(across)
        for axis, slots in (("dp", tile_slots), ("row", row_slots)):
            slot = slots.at[me[axis]]
            slot[...] = value.astype(slots.dtype)
            for d in peers(axis):
                post(copies, slot, slot, axis, d)
            yield
            settle(copies)
            value = total_of(slots)
        full[mine, :] = value.astype(full.dtype)
        for d in peers("col"):
            post(copies, full.at[mine], full.at[mine], "col", d)
        yield
        settle(copies)

    def loop(steps, body, init=0):
        return lax.fori_loop(0, steps, body, init)

    def cat(ref, at, count, low=None, high=None):
        part = slice(low, high)
        return jnp.concatenate([ref[at + k, part, :] for k in range(count)], axis=1)

    def spread_rows(ref, at, value, low=None, high=None):
        for k in range(value.shape[1] // cols):
            ref[at + k, low:high, :] = value[:, k * cols:(k + 1) * cols]

    def clear_edges(n, field, depth):
        blank = jnp.zeros((depth, cols), BF16)

        @pl.when(jnp.logical_not(exists("row", -1)))
        def _():
            field[0, depth:2 * depth, :] = blank

        @pl.when(jnp.logical_not(exists("row", 1)))
        def _():
            field[rows + 1, depth:2 * depth, :] = blank

        for side in range(2):
            @pl.when(jnp.logical_not(exists("col", 1 if side else -1)))
            def _():
                got[n][side] = blank

    def send_rows(n, field, depth):
        down = push(
            field.at[rows, pl.ds(depth, depth)], field.at[0, pl.ds(depth, depth)], "row", 1
        )
        up = push(
            field.at[1, pl.ds(depth, depth)],
            field.at[rows + 1, pl.ds(depth, depth)], "row", -1,
        )
        return down, up

    def publish(n, field, depth, at, value):
        lane = lax.broadcasted_iota(jnp.int32, (depth, cols), 1) // 2
        for k in range(value.shape[1] // cols):
            row = value[:, k * cols:(k + 1) * cols]
            i = at + k
            field[i, depth:2 * depth, :] = row
            field[i, :depth, :] = pltpu.roll(row, 1, 1)
            field[i, 2 * depth:, :] = pltpu.roll(row, cols - 1, 1)
            strips[n][...] = jnp.where(lane == i, pltpu.roll(row, 2 * i + 1, 1), strips[n][...])

    def send_strip(n, field, depth, held):
        for wait in held:
            wait()
        for i in (0, rows + 1):
            publish(n, field, depth, i, field[i, depth:2 * depth, :])
        right = push(strips[n], got[n].at[0], "col", 1)
        left = push(strips[n], got[n].at[1], "col", -1)
        return right, left

    def widen(n, field, depth, held):
        for wait in held:
            wait()
        lane = lax.broadcasted_iota(jnp.int32, (depth, cols), 1)
        before, after = got[n][0], got[n][1]
        for i in range(rows + 2):
            field[i, :depth, :] = jnp.where(
                lane == 0, pltpu.roll(before, (cols - 2 * i) % cols, 1), field[i, :depth, :]
            )
            field[i, 2 * depth:, :] = jnp.where(
                lane == cols - 1, pltpu.roll(after, (cols - 2 - 2 * i) % cols, 1),
                field[i, 2 * depth:, :],
            )

    def conv(weight, field, at):
        return sum(dot(weight(dy), cat(field, at + dy, GROUP)) for dy in range(3))

    def sweep(body, between, init=0, halfway=None):
        groups = rows // GROUP
        carry = loop(2, lambda j, c: body(j * (groups - 1), c), init)
        held = between()
        half = groups // 2 - 1
        carry = loop(half, lambda j, c: body(j + 1, c), carry)
        if halfway is not None:
            halfway()
        return held, loop(groups - 2 - half, lambda j, c: body(j + 1 + half, c), carry)

    fields = [(first, mid), (block, chans), (dlog, outs), (dsec, mid)]
    for n, (field, depth) in enumerate(fields):
        clear_edges(n, field, depth)
        strips[n][...] = jnp.zeros((depth, cols), BF16)
    for ref in (dzero, dsec_zero):
        ref[0] = jnp.zeros(ref.shape[1:], BF16)
        ref[rows + 1] = jnp.zeros(ref.shape[1:], BF16)
    for ref in (acc_c, acc_s, acc_e, acc_r):
        ref[...] = jnp.zeros_like(ref)
    big_send[...] = jnp.zeros_like(big_send)
    pl.semaphore_wait(barrier, sum(sizes[axis] - 1 for axis in AXES))

    def make_first(i, c):
        z = dot(wr_ref[...], cat(x_ref, i * GROUP, GROUP))
        publish(0, first, mid, i * GROUP + 1, jnp.maximum(z, 0.0).astype(BF16))
        return c

    held, _ = sweep(make_first, lambda: send_rows(0, first, mid))
    for dy in range(3):
        for dx in range(3):
            ws_ref[dy, :, dx * mid:(dx + 1) * mid] = spatial_ref[dy, dx]
            wc_ref[dy, dx, :heads, :] = class_ref[dy, dx]
            wc_ref[dy, dx, heads:, :] = jnp.zeros((outs - heads, chans), BF16)
    for h in range(rows):
        code = jnp.where(mask_ref[:, h, :] > 0, label_ref[:, h, :], 64)
        code_ref[h, :A, :] = code.astype(F32).astype(BF16)
        code_ref[h, A:, :] = jnp.ones((16 - A, cols), BF16)
    held = send_strip(0, first, mid, held)

    def turned(parts):
        size = parts[0].shape[1]
        eye = jnp.where(
            lax.broadcasted_iota(jnp.int32, (size, size), 0)
            == lax.broadcasted_iota(jnp.int32, (size, size), 1), 1.0, 0.0,
        ).astype(BF16)
        return dot_t(eye, jnp.concatenate(parts, axis=0)).astype(BF16)

    wet_ref[...] = turned([we_ref[...]])
    for dy in range(3):
        wsb_ref[dy] = turned([spatial_ref[2 - dy, 2 - dx] for dx in range(3)])
        wcb_ref[dy] = turned([wc_ref[2 - dy, 2 - dx] for dx in range(3)])
    widen(0, first, mid, held)

    def make_block(i, c):
        s = jnp.maximum(conv(lambda dy: ws_ref[dy], first, i * GROUP), 0.0).astype(BF16)
        spread_rows(second, i * GROUP, s)
        b = jnp.maximum(cat(x_ref, i * GROUP, GROUP).astype(F32) + dot(we_ref[...], s), 0.0)
        publish(1, block, chans, i * GROUP + 1, b.astype(BF16))
        return c

    held, _ = sweep(make_block, lambda: send_rows(1, block, chans))
    held = send_strip(1, block, chans, held)
    widen(1, block, chans, held)

    def class_rows(dy):
        return jnp.concatenate([wc_ref[dy, dx] for dx in range(3)], axis=1)

    def make_dlog(i, carry):
        total, count = carry
        z = conv(class_rows, block, i * GROUP)
        code = cat(code_ref, i * GROUP, GROUP)
        gap = dot(spread_ref[...], code)
        target = gap == 0.0
        alpha = jnp.where(target, 0.25, jnp.where(gap > 32.0, 0.0, 0.75))
        z = z * LOG2E
        u = jnp.where(target, -z, z)
        e = jnp.exp2(-jnp.abs(u))
        soft = jnp.maximum(u, 0.0) + jnp.log2(1.0 + e)
        prob = jnp.exp2(u - soft)
        scaled = alpha * prob * prob
        total = total + jnp.sum(scaled * soft, axis=0, keepdims=True)
        slope = scaled * ((2.0 * LN2 - 2.0 * LN2 * prob) * soft + prob)
        d = jnp.where(target, -slope, slope).astype(BF16)
        publish(2, dlog, outs, i * GROUP + 1, d)
        spread_rows(dzero, i * GROUP + 1, d)
        codes = code.astype(F32)
        row = lax.broadcasted_iota(jnp.int32, codes.shape, 0)
        hit = jnp.where((codes > 0.5) & (codes < 32.0) & (row < A), 1.0, 0.0)
        count = count + jnp.sum(hit, axis=0, keepdims=True)
        return total, count

    zero = jnp.zeros((1, GROUP * cols), F32)
    held, (total, count) = sweep(make_dlog, lambda: send_rows(2, dlog, outs), (zero, zero))
    fold = lambda v: sum(v[:, k * 128:(k + 1) * 128] for k in range(v.shape[1] // 128))
    stat[0:1, :] = fold(total) * LN2
    stat[1:2, :] = fold(count)
    stat[2:, :] = jnp.zeros((6, 128), F32)
    stats = reduce_stats()
    next(stats)

    def weight_sum(acc, grad, field):
        depth = grad.shape[1]

        def add(i, c):
            at = i * WIDE + 1
            tall = jnp.concatenate([cat(grad, at + 1 - dy, WIDE) for dy in range(3)], axis=0)
            acc[...] += dot_t(tall, cat(field, at, WIDE))
            return c

        loop(rows // WIDE, add)
        acc[:depth, :] += dot_t(grad[1], field[0])
        acc[2 * depth:, :] += dot_t(grad[rows], field[rows + 1])

    def advance(*steps):
        for step in steps:
            next(step, None)

    weight_sum(acc_c, dzero, block)
    share = big_send.shape[0] // 3
    for dy in range(3):
        for dx in range(3):
            at = dy * share + dx * outs
            big_send[at:at + outs, :] = acc_c[
                dy * outs:(dy + 1) * outs, dx * chans:(dx + 1) * chans
            ].astype(BF16)
    big = reduce_big(orders)
    advance(big, stats)
    held = send_strip(2, dlog, outs, held)
    widen(2, dlog, outs, held)

    def make_dsec(i, c):
        g = conv(lambda dy: wcb_ref[dy], dlog, i * GROUP)
        b = cat(block, i * GROUP + 1, GROUP, chans, 2 * chans).astype(F32)
        ds = jnp.where(b > 0.0, g, 0.0).astype(BF16)
        s = cat(second, i * GROUP, GROUP)
        acc_e[...] += dot_t(s, ds)
        h = dot(wet_ref[...], ds)
        d = jnp.where(s.astype(F32) > 0.0, h, 0.0).astype(BF16)
        publish(3, dsec, mid, i * GROUP + 1, d)
        spread_rows(dsec_zero, i * GROUP + 1, d)
        return c

    def after_edges():
        sent = send_rows(3, dsec, mid)
        advance(big, stats)
        return sent

    held, _ = sweep(make_dsec, after_edges, halfway=lambda: advance(big, stats))
    advance(big)
    weight_sum(acc_s, dsec_zero, first)
    held = send_strip(3, dsec, mid, held)
    mid_send, mid_full = mid_refs[:2]
    mid_send[:mid, :] = acc_e[...].astype(mid_send.dtype)
    mid_send[mid:, :] = jnp.zeros((mid_send.shape[0] - mid, chans), mid_send.dtype)
    mid_send[mid:4 * mid, :3 * mid] = acc_s[...].astype(mid_send.dtype)
    middle = reduce_small(mid_refs)
    advance(middle)
    widen(3, dsec, mid, held)
    advance(big, middle)

    def make_dfirst(i, c):
        g = conv(lambda dy: wsb_ref[dy], dsec, i * GROUP)
        f = cat(first, i * GROUP + 1, GROUP, mid, 2 * mid).astype(F32)
        df = jnp.where(f > 0.0, g, 0.0).astype(BF16)
        acc_r[...] += dot_t(df, cat(x_ref, i * GROUP, GROUP))
        return c

    loop(rows // GROUP, make_dfirst)
    tail_send, tail_full = tail_refs[:2]
    tail_send[:mid, :] = acc_r[...].astype(tail_send.dtype)
    if tail_send.shape[0] > mid:
        tail_send[mid:, :] = jnp.zeros((tail_send.shape[0] - mid, chans), tail_send.dtype)
    tail = reduce_small(tail_refs)
    advance(tail, big, middle)
    scale = 1.0 / jnp.sum(stat[1:2, :], axis=1, keepdims=True)
    loss_ref[...] = jnp.sum(stat[0:1, :], axis=1, keepdims=True) * scale
    advance(tail, middle)
    advance(big)
    for dy in range(3):
        for dx in range(3):
            at = dy * share + dx * outs
            grad_class_ref[dy, dx] = big_full[at:at + outs, :].astype(F32)[:heads] * scale
    advance(tail, middle)
    grad_expand_ref[...] = (mid_full[:mid, :].astype(F32) * scale).T
    for dy in range(3):
        part = mid_full[(dy + 1) * mid:(dy + 2) * mid, :].astype(F32) * scale
        for dx in range(3):
            grad_spatial_ref[dy, dx] = part[:, dx * mid:(dx + 1) * mid]
    advance(tail)
    advance(tail)
    grad_reduce_ref[...] = tail_full[:mid, :].astype(F32) * scale


def per_device(
    inputs, reduce_weight, spatial_weight, expand_weight, class_weight, anchor_labels, anchor_mask
):
    tiles, chans, rows, cols = inputs.shape
    assert tiles == 1
    mid = reduce_weight.shape[0]
    heads = class_weight.shape[2]
    outs = -(-heads // 16) * 16
    sizes = {axis: lax.axis_size(axis) for axis in AXES}

    x = inputs[0].transpose(1, 0, 2)

    spread = np.zeros((outs, 16), np.float32)
    spread[np.arange(heads), np.arange(heads) // K] = 1.0
    spread[np.arange(heads), A] = -1.0 - np.arange(heads) % K
    spread[heads:, A] = 64.0
    spread = jnp.asarray(spread, BF16)

    depths = (mid, chans, outs, mid)
    orders = [AXES[s:] + AXES[:s] for s in range(len(AXES))]
    devices = int(np.prod([sizes[axis] for axis in AXES]))
    share = -(-3 * outs // (16 * devices)) * 16 * devices

    def slots(order):
        size, out = share, []
        for axis in order:
            size //= sizes[axis]
            out.append(pltpu.VMEM((max(sizes[axis] - 1, 1), size, chans), BF16))
        return out

    def small(need, kind):
        piece = -(-need // (16 * sizes["col"])) * 16
        full = pltpu.VMEM((piece * sizes["col"], chans), kind)
        return [full, full] + [
            pltpu.VMEM((sizes[axis], piece, chans), kind) for axis in ("col", "dp", "row")
        ]

    copies = 16 + sum(
        (sizes[axis] - 1) * (1 + 2 * len(orders) + 2 * (2 if axis == "col" else 1))
        for axis in AXES
    )
    outputs = [(1, 1), (mid, chans), (3, 3, mid, mid), (chans, mid), class_weight.shape]

    loss, *grads = pl.pallas_call(
        functools.partial(step_kernel, sizes, orders, heads),
        out_shape=[jax.ShapeDtypeStruct(shape, F32) for shape in outputs],
        in_specs=[pl.BlockSpec(memory_space=pltpu.VMEM)] * 8,
        out_specs=[pl.BlockSpec(memory_space=pltpu.VMEM)] * 5,
        scratch_shapes=[
            pltpu.VMEM((rows + 2, 3 * mid, cols), BF16),
            pltpu.VMEM((rows, mid, cols), BF16),
            pltpu.VMEM((rows + 2, 3 * chans, cols), BF16),
            pltpu.VMEM((rows + 2, 3 * outs, cols), BF16),
            pltpu.VMEM((rows + 2, outs, cols), BF16),
            pltpu.VMEM((rows + 2, 3 * mid, cols), BF16),
            pltpu.VMEM((rows + 2, mid, cols), BF16),
            pltpu.VMEM((3 * outs, 3 * chans), F32),
            pltpu.VMEM((3 * mid, 3 * mid), F32),
            pltpu.VMEM((mid, chans), F32),
            pltpu.VMEM((mid, chans), F32),
            pltpu.VMEM((rows, 16, cols), BF16),
            pltpu.VMEM((3, mid, 3 * mid), BF16),
            pltpu.VMEM((3, mid, 3 * mid), BF16),
            pltpu.VMEM((mid, chans), BF16),
            pltpu.VMEM((3, 3, outs, chans), BF16),
            pltpu.VMEM((3, chans, 3 * outs), BF16),
            [pltpu.VMEM((depth, cols), BF16) for depth in depths],
            [pltpu.VMEM((2, depth, cols), BF16) for depth in depths],
            pltpu.VMEM((8, 128), F32),
            [pltpu.VMEM((sizes[axis], 8, 128), F32) for axis in AXES],
            pltpu.VMEM((3 * share, chans), BF16),
            pltpu.VMEM((3 * share, chans), F32),
            pltpu.VMEM((3 * share, chans), BF16),
            [slots(order) for order in orders],
            small(4 * mid, BF16),
            small(mid, F32),
            pltpu.SemaphoreType.DMA((copies,)),
            pltpu.SemaphoreType.DMA((copies,)),
        ],
        compiler_params=pltpu.CompilerParams(
            collective_id=1, has_side_effects=True, vmem_limit_bytes=60 * 1024 * 1024
        ),
        name="tile_step",
    )(
        x, anchor_labels[0], anchor_mask[0], spread, reduce_weight, spatial_weight,
        expand_weight, class_weight,
    )
    return loss.reshape(()), *grads


def solution(mesh):
    tiled = P("dp", None, "row", "col")
    return jax.shard_map(
        per_device,
        mesh=mesh,
        in_specs=(tiled, P(), P(), P(), P(), tiled, tiled),
        out_specs=(P(), P(), P(), P(), P()),
        check_vma=False,
    )
```

time: 97.9 us -> 92.1 us (0.941)
  Pallas kernels: 83 us -> 76.9 us
  local copies, waits for them, and re-layouts: 9.41 us -> 12.5 us
  between operations: 3.83 us -> 2.41 us
  other arithmetic: 1.36 us -> 0 us
    pallas_call x2 -> x1, Pallas kernels: 83 us -> 76.9 us  [per_device(): pl.pallas_call(functools.partial(step_kernel, sizes, orders, heads), out_...]
    unnamed x7 -> x6, local copies, waits for them, and re-layouts: 8.06 us -> 12.5 us
    mul x2 -> x0, local copies, waits for them, and re-layouts: 1.35 us -> none  [the longest x1 1.19 us: finish(): pack[:9 * heads].reshape(3, 3, heads, chans) * scale]
where the time goes in v3:
time: 92.1 us; the launch traced here: 91.7 us
  Pallas kernels  76.9 us (83%)
  local copies, waits for them, and re-layouts  12.5 us (14%)
  between operations  2.41 us (3%)
    pallas_call x1, Pallas kernels, per_device(): pl.pallas_call(functools.partial(step_kernel, sizes, orders, heads), out_...  76.9 us
    unnamed x6, local copies, waits for them, and re-layouts  12.5 us

profile of v3, /device:TPU:0, one launch (start us, length us, event | category | flops | bytes accessed | tf_op | source)
XLA Modules:
  0.0 91.7 jit_solution(15306254573727137926)
XLA Ops:
  0.6 1.5 %copy.14.we_ref = bf16[256,64]{1,0:T(8,128)(2,1)} copy(bf16[256,64]{0,1:T(8,128)(2,1)} %param.11) | data formatting | bytes 65536 | tf_op args[3]
  2.1 3.7 %copy.17 = bf16[1,256,32,128]{3,1,2,0:T(8,128)(2,1)} copy(bf16[1,256,32,128]{3,2,1,0:T(8,128)(2,1)} %param.8) | data formatting | bytes 4194304 | tf_op args[0]
  5.9 76.9 %tile_step.1 = (f32[1,1]{1,0:T(1,128)}, f32[64,256]{1,0:T(8,128)}, f32[3,3,64,64]{3,2,1,0:T(8,128)}, f32[256,64]{1,0:T(8,128)}, f32[3,3,135,256]{3,2,1,0:T(8,128)}) custom-call(bf16[32,256,128]{2,1,0:T(8,128)(2,1)} %bitcast.8, s32[9,32,128]{2,1,0:T(8,128)} %bitcast.9, s32[9,32,128]{2,1,0:T(8,128)} %bitcast.10, bf16[144,16]{1,0:T(8,128)(2,1)} %constant.2.clone.spread_ref, ...), custom_call_target="tpu_custom_call" | custom-call | tf_op jit(solution)/shard_map/tile_step/pallas_call | solution.py:481
  82.8 1.6 %copy.15 = f32[256,64]{0,1:T(8,128)} copy(f32[256,64]{1,0:T(8,128)} %get-tuple-element.18) | data formatting | bytes 131072
  85.0 1.5 %copy.23 = f32[64,256]{1,0:T(8,128)} copy(f32[64,256]{1,0:T(8,128)} %get-tuple-element.26) | data formatting | bytes 131072
  86.5 1.7 %copy.24 = f32[3,3,64,64]{3,2,1,0:T(8,128)} copy(f32[3,3,64,64]{3,2,1,0:T(8,128)} %get-tuple-element.27) | data formatting | bytes 294912
  88.2 2.4 %copy.25 = f32[3,3,135,256]{3,2,1,0:T(8,128)} copy(f32[3,3,135,256]{3,2,1,0:T(8,128)} %get-tuple-element.29) | data formatting | bytes 2488320

commit v4 on v3

--- a/solution.py
+++ b/solution.py
@@ -28,12 +28,12 @@
 
 
 def step_kernel(
-    sizes, orders, heads,
-    x_ref, label_ref, mask_ref, spread_ref, wr_ref, spatial_ref, we_ref, class_ref,
-    loss_ref, grad_reduce_ref, grad_spatial_ref, grad_expand_ref, grad_class_ref,
+    sizes, heads,
+    x_ref, label_ref, mask_ref, spread_ref, wr_ref, spatial_ref, wet_ref, class_ref,
+    loss_ref, scale_ref, small_out, spatial_out, class_out,
     first, second, block, dlog, dzero, dsec, dsec_zero, acc_c, acc_s, acc_e, acc_r,
-    code_ref, ws_ref, wsb_ref, wet_ref, wc_ref, wcb_ref, strips, got,
-    stat, stat_slots, big_send, big_work, big_full, big_slots, mid_refs, tail_refs, ssem, rsem,
+    code_ref, ws_ref, wsb_ref, we_ref, wc_ref, wcb_ref, strips, got,
+    stat, stat_slots, big_refs, mid_refs, tail_refs, ssem, rsem, osem,
 ):
     rows, chans, cols = x_ref.shape
     mid = wr_ref.shape[0]
@@ -46,24 +46,28 @@
     def exists(axis, step):
         return me[axis] < sizes[axis] - 1 if step > 0 else me[axis] > 0
 
+    plane = [
+        (d, e) for d in range(sizes["dp"]) for e in range(sizes["col"]) if d or e
+    ]
+    shift = lambda axis, d: lax.rem(me[axis] + d, sizes[axis])
+    across = [{"dp": shift("dp", d), "col": shift("col", e)} for d, e in plane]
+    along = [{"row": shift("row", d)} for d in peers("row")]
+    place = lambda to: to["dp"] * sizes["col"] + to["col"]
+
     barrier = pltpu.get_barrier_semaphore()
-    for axis in AXES:
-        for d in peers(axis):
-            pl.semaphore_signal(
-                barrier, inc=1, device_id={axis: lax.rem(me[axis] + d, sizes[axis])},
-                device_id_type=mesh_id,
-            )
-
-    def remote(src, dst, axis, to):
+    for to in across + along:
+        pl.semaphore_signal(barrier, inc=1, device_id=to, device_id_type=mesh_id)
+
+    def remote(src, dst, to):
         n = used[0]
         used[0] += 1
         return pltpu.make_async_remote_copy(
             src_ref=src, dst_ref=dst, send_sem=ssem.at[n], recv_sem=rsem.at[n],
-            device_id={axis: to}, device_id_type=mesh_id,
+            device_id=to, device_id_type=mesh_id,
         )
 
     def push(src, dst, axis, step):
-        copy = remote(src, dst, axis, me[axis] + step)
+        copy = remote(src, dst, {axis: me[axis] + step})
 
         @pl.when(exists(axis, step))
         def _():
@@ -80,94 +84,54 @@
 
         return finish
 
-    def post(copies, src, dst, axis, d):
-        copy = remote(src, dst, axis, lax.rem(me[axis] + d, sizes[axis]))
-        copy.start()
-        copies.append(copy)
-
     def settle(copies):
         for copy in copies:
             copy.wait()
-        copies.clear()
 
     def total_of(slots):
         return sum(slots[j].astype(F32) for j in range(slots.shape[0]))
 
-    def reduce_stats():
-        copies = []
-        value = stat[...]
-        for k, axis in enumerate(AXES):
-            slot = stat_slots[k].at[me[axis]]
-            slot[...] = value
-            for d in peers(axis):
-                post(copies, slot, slot, axis, d)
-            yield
-            settle(copies)
-            value = total_of(stat_slots[k])
-        stat[...] = value
-
-    def reduce_big(orders):
-        share = big_send.shape[0] // len(orders)
-        base = [s * share for s in range(len(orders))]
-        copies = []
-        part = lambda s, rows: pl.ds(pl.multiple_of(base[s], 16), rows)
-        for k in range(len(AXES)):
-            for s, order in enumerate(orders):
-                axis, piece = order[k], big_slots[s][k].shape[1]
-                for d in peers(axis):
-                    to = lax.rem(me[axis] + d, sizes[axis])
-                    src = big_send.at[pl.ds(pl.multiple_of(base[s] + to * piece, 16), piece)]
-                    post(copies, src, big_slots[s][k].at[d - 1], axis, d)
-            yield
-            settle(copies)
-            for s, order in enumerate(orders):
-                axis, piece = order[k], big_slots[s][k].shape[1]
-                base[s] = base[s] + me[axis] * piece
-                at = part(s, piece)
-                value = (big_work if k else big_send)[at, :].astype(F32)
-                for d in peers(axis):
-                    value = value + big_slots[s][k][d - 1].astype(F32)
-                if k < len(AXES) - 1:
-                    big_work[at, :] = value
-                    big_send[at, :] = value.astype(BF16)
-                else:
-                    big_full[at, :] = value.astype(BF16)
-        for k in reversed(range(len(AXES))):
-            for s, order in enumerate(orders):
-                axis, piece = order[k], big_slots[s][k].shape[1]
-                at = part(s, piece)
-                for d in peers(axis):
-                    post(copies, big_full.at[at], big_full.at[at], axis, d)
-                base[s] = base[s] - me[axis] * piece
-            yield
-            settle(copies)
-
-    def reduce_small(refs):
-        send, full, across, tile_slots, row_slots = refs
-        piece = across.shape[1]
-        copies = []
-        mine = pl.ds(pl.multiple_of(me["col"] * piece, 16), piece)
-        across[me["col"]] = send[mine, :]
-        for d in peers("col"):
-            to = lax.rem(me["col"] + d, sizes["col"])
-            src = send.at[pl.ds(pl.multiple_of(to * piece, 16), piece)]
-            post(copies, src, across.at[me["col"]], "col", d)
+    def share_all(slots, value, targets, mine):
+        slot = slots.at[mine]
+        slot[...] = value.astype(slots.dtype)
+        copies = [remote(slot, slot, to) for to in targets]
+        for copy in copies:
+            copy.start()
+        return copies
+
+    def reduce_whole(value, plane_slots, row_slots, store):
+        copies = share_all(plane_slots, value, across, place(me))
         yield
         settle(copies)
-        value = total_of(across)
-        for axis, slots in (("dp", tile_slots), ("row", row_slots)):
-            slot = slots.at[me[axis]]
-            slot[...] = value.astype(slots.dtype)
-            for d in peers(axis):
-                post(copies, slot, slot, axis, d)
-            yield
-            settle(copies)
-            value = total_of(slots)
-        full[mine, :] = value.astype(full.dtype)
-        for d in peers("col"):
-            post(copies, full.at[mine], full.at[mine], "col", d)
+        copies = share_all(row_slots, total_of(plane_slots), along, me["row"])
         yield
         settle(copies)
+        store(total_of(row_slots))
+
+    def reduce_split(refs):
+        send, full, plane_slots, row_slots = refs
+        piece = row_slots.shape[1]
+        part = lambda to: pl.ds(pl.multiple_of(place(to) * piece, 16), piece)
+        slot = plane_slots.at[place(me)]
+        slot[...] = send[part(me), :]
+        copies = [remote(send.at[part(to)], slot, to) for to in across]
+        for copy in copies:
+            copy.start()
+        yield
+        settle(copies)
+        copies = share_all(row_slots, total_of(plane_slots), along, me["row"])
+        yield
+        settle(copies)
+        full[part(me), :] = total_of(row_slots).astype(full.dtype)
+        copies = [remote(full.at[part(me)], full.at[part(me)], to) for to in across]
+        for copy in copies:
+            copy.start()
+        yield
+        settle(copies)
+
+    def advance(*steps):
+        for step in steps:
+            next(step, None)
 
     def loop(steps, body, init=0):
         return lax.fori_loop(0, steps, body, init)
@@ -259,10 +223,9 @@
     for ref in (dzero, dsec_zero):
         ref[0] = jnp.zeros(ref.shape[1:], BF16)
         ref[rows + 1] = jnp.zeros(ref.shape[1:], BF16)
-    for ref in (acc_c, acc_s, acc_e, acc_r):
+    for ref in (acc_e, acc_r, mid_refs[0]) + tuple(refs[0] for refs in big_refs):
         ref[...] = jnp.zeros_like(ref)
-    big_send[...] = jnp.zeros_like(big_send)
-    pl.semaphore_wait(barrier, sum(sizes[axis] - 1 for axis in AXES))
+    pl.semaphore_wait(barrier, len(across) + len(along))
 
     def make_first(i, c):
         z = dot(wr_ref[...], cat(x_ref, i * GROUP, GROUP))
@@ -289,7 +252,7 @@
         ).astype(BF16)
         return dot_t(eye, jnp.concatenate(parts, axis=0)).astype(BF16)
 
-    wet_ref[...] = turned([we_ref[...]])
+    we_ref[...] = turned([wet_ref[...]])
     for dy in range(3):
         wsb_ref[dy] = turned([spatial_ref[2 - dy, 2 - dx] for dx in range(3)])
         wcb_ref[dy] = turned([wc_ref[2 - dy, 2 - dx] for dx in range(3)])
@@ -339,37 +302,36 @@
     stat[0:1, :] = fold(total) * LN2
     stat[1:2, :] = fold(count)
     stat[2:, :] = jnp.zeros((6, 128), F32)
-    stats = reduce_stats()
-    next(stats)
-
-    def weight_sum(acc, grad, field):
+
+    def keep(value):
+        stat[...] = value
+
+    stats = reduce_whole(stat[...], *stat_slots, keep)
+    advance(stats)
+    held = send_strip(2, dlog, outs, held)
+
+    def weight_sum(acc, grad, field, low, high):
         depth = grad.shape[1]
+        acc[...] = jnp.zeros_like(acc)
 
         def add(i, c):
             at = i * WIDE + 1
             tall = jnp.concatenate([cat(grad, at + 1 - dy, WIDE) for dy in range(3)], axis=0)
-            acc[...] += dot_t(tall, cat(field, at, WIDE))
+            acc[...] += dot_t(tall, cat(field, at, WIDE, low, high))
             return c
 
         loop(rows // WIDE, add)
-        acc[:depth, :] += dot_t(grad[1], field[0])
-        acc[2 * depth:, :] += dot_t(grad[rows], field[rows + 1])
-
-    def advance(*steps):
-        for step in steps:
-            next(step, None)
-
-    weight_sum(acc_c, dzero, block)
-    share = big_send.shape[0] // 3
-    for dy in range(3):
-        for dx in range(3):
-            at = dy * share + dx * outs
-            big_send[at:at + outs, :] = acc_c[
-                dy * outs:(dy + 1) * outs, dx * chans:(dx + 1) * chans
-            ].astype(BF16)
-    big = reduce_big(orders)
-    advance(big, stats)
-    held = send_strip(2, dlog, outs, held)
+        acc[:depth, :] += dot_t(grad[1], field[0, low:high])
+        acc[2 * depth:, :] += dot_t(grad[rows], field[rows + 1, low:high])
+
+    bigs = []
+    for dx in range(3):
+        low, high = dx * chans, (dx + 1) * chans
+        weight_sum(acc_c, dzero, block, low, high)
+        send = big_refs[dx][0]
+        send[:3 * outs, :] = acc_c[...].astype(BF16)
+        bigs.append(reduce_split(big_refs[dx]))
+        advance(bigs[dx])
     widen(2, dlog, outs, held)
 
     def make_dsec(i, c):
@@ -386,21 +348,21 @@
 
     def after_edges():
         sent = send_rows(3, dsec, mid)
-        advance(big, stats)
+        advance(bigs[0], stats)
         return sent
 
-    held, _ = sweep(make_dsec, after_edges, halfway=lambda: advance(big, stats))
-    advance(big)
-    weight_sum(acc_s, dsec_zero, first)
+    held, _ = sweep(make_dsec, after_edges, halfway=lambda: advance(*bigs[1:]))
     held = send_strip(3, dsec, mid, held)
+    advance(bigs[0], stats)
+    weight_sum(acc_s, dsec_zero, first, 0, 3 * mid)
     mid_send, mid_full = mid_refs[:2]
-    mid_send[:mid, :] = acc_e[...].astype(mid_send.dtype)
-    mid_send[mid:, :] = jnp.zeros((mid_send.shape[0] - mid, chans), mid_send.dtype)
-    mid_send[mid:4 * mid, :3 * mid] = acc_s[...].astype(mid_send.dtype)
-    middle = reduce_small(mid_refs)
+    mid_send[:mid, :] = acc_e[...].astype(BF16)
+    mid_send[mid:4 * mid, :3 * mid] = acc_s[...].astype(BF16)
+    middle = reduce_split(mid_refs)
     advance(middle)
+    advance(bigs[1])
     widen(3, dsec, mid, held)
-    advance(big, middle)
+    advance(bigs[2])
 
     def make_dfirst(i, c):
         g = conv(lambda dy: wsb_ref[dy], dsec, i * GROUP)
@@ -410,29 +372,33 @@
         return c
 
     loop(rows // GROUP, make_dfirst)
-    tail_send, tail_full = tail_refs[:2]
-    tail_send[:mid, :] = acc_r[...].astype(tail_send.dtype)
-    if tail_send.shape[0] > mid:
-        tail_send[mid:, :] = jnp.zeros((tail_send.shape[0] - mid, chans), tail_send.dtype)
-    tail = reduce_small(tail_refs)
-    advance(tail, big, middle)
+
+    def place_tail(value):
+        small_out[:mid, :] = value
+
+    tail = reduce_whole(acc_r[...], *tail_refs, place_tail)
+    advance(tail, middle, *bigs)
+    outgoing = []
+    for dx in range(3):
+        for dy in range(3):
+            outgoing.append(pltpu.make_async_copy(
+                big_refs[dx][1].at[pl.ds(dy * outs, outs)], class_out.at[dy, dx],
+                osem.at[3 * dx + dy],
+            ))
+            outgoing[-1].start()
     scale = 1.0 / jnp.sum(stat[1:2, :], axis=1, keepdims=True)
+    scale_ref[...] = scale
     loss_ref[...] = jnp.sum(stat[0:1, :], axis=1, keepdims=True) * scale
     advance(tail, middle)
-    advance(big)
+    advance(middle)
+    small_out[mid:, :] = mid_full[:mid, :].astype(F32)
     for dy in range(3):
+        part = mid_full[(dy + 1) * mid:(dy + 2) * mid, :].astype(F32)
         for dx in range(3):
-            at = dy * share + dx * outs
-            grad_class_ref[dy, dx] = big_full[at:at + outs, :].astype(F32)[:heads] * scale
-    advance(tail, middle)
-    grad_expand_ref[...] = (mid_full[:mid, :].astype(F32) * scale).T
-    for dy in range(3):
-        part = mid_full[(dy + 1) * mid:(dy + 2) * mid, :].astype(F32) * scale
-        for dx in range(3):
-            grad_spatial_ref[dy, dx] = part[:, dx * mid:(dx + 1) * mid]
+            spatial_out[dy, dx] = part[:, dx * mid:(dx + 1) * mid]
     advance(tail)
-    advance(tail)
-    grad_reduce_ref[...] = tail_full[:mid, :].astype(F32) * scale
+    for copy in outgoing:
+        copy.wait()
 
 
 def per_device(
@@ -454,35 +420,30 @@
     spread = jnp.asarray(spread, BF16)
 
     depths = (mid, chans, outs, mid)
-    orders = [AXES[s:] + AXES[:s] for s in range(len(AXES))]
-    devices = int(np.prod([sizes[axis] for axis in AXES]))
-    share = -(-3 * outs // (16 * devices)) * 16 * devices
-
-    def slots(order):
-        size, out = share, []
-        for axis in order:
-            size //= sizes[axis]
-            out.append(pltpu.VMEM((max(sizes[axis] - 1, 1), size, chans), BF16))
-        return out
-
-    def small(need, kind):
-        piece = -(-need // (16 * sizes["col"])) * 16
-        full = pltpu.VMEM((piece * sizes["col"], chans), kind)
+    across = sizes["dp"] * sizes["col"]
+
+    def split_refs(need):
+        piece = -(-need // (16 * across)) * 16
+        full = pltpu.VMEM((piece * across, chans), BF16)
         return [full, full] + [
-            pltpu.VMEM((sizes[axis], piece, chans), kind) for axis in ("col", "dp", "row")
+            pltpu.VMEM((count, piece, chans), BF16) for count in (across, sizes["row"])
         ]
 
-    copies = 16 + sum(
-        (sizes[axis] - 1) * (1 + 2 * len(orders) + 2 * (2 if axis == "col" else 1))
-        for axis in AXES
-    )
-    outputs = [(1, 1), (mid, chans), (3, 3, mid, mid), (chans, mid), class_weight.shape]
-
-    loss, *grads = pl.pallas_call(
-        functools.partial(step_kernel, sizes, orders, heads),
-        out_shape=[jax.ShapeDtypeStruct(shape, F32) for shape in outputs],
+    def whole_refs(shape, kind):
+        return [pltpu.VMEM((count,) + shape, kind) for count in (across, sizes["row"])]
+
+    copies = 16 + 6 * (across - 1) + 4 * (across - 1) + 6 * (sizes["row"] - 1)
+    outputs = [
+        ((1, 1), F32), ((1, 1), F32), ((2 * mid, chans), F32), ((3, 3, mid, mid), F32),
+        ((3, 3, outs, chans), BF16),
+    ]
+
+    loss, scale, small, spatial, wide = pl.pallas_call(
+        functools.partial(step_kernel, sizes, heads),
+        out_shape=[jax.ShapeDtypeStruct(*output) for output in outputs],
         in_specs=[pl.BlockSpec(memory_space=pltpu.VMEM)] * 8,
-        out_specs=[pl.BlockSpec(memory_space=pltpu.VMEM)] * 5,
+        out_specs=[pl.BlockSpec(memory_space=pltpu.VMEM)] * 4
+        + [pl.BlockSpec(memory_space=pl.ANY)],
         scratch_shapes=[
             pltpu.VMEM((rows + 2, 3 * mid, cols), BF16),
             pltpu.VMEM((rows, mid, cols), BF16),
@@ -491,28 +452,26 @@
             pltpu.VMEM((rows + 2, outs, cols), BF16),
             pltpu.VMEM((rows + 2, 3 * mid, cols), BF16),
             pltpu.VMEM((rows + 2, mid, cols), BF16),
-            pltpu.VMEM((3 * outs, 3 * chans), F32),
+            pltpu.VMEM((3 * outs, chans), F32),
             pltpu.VMEM((3 * mid, 3 * mid), F32),
             pltpu.VMEM((mid, chans), F32),
             pltpu.VMEM((mid, chans), F32),
             pltpu.VMEM((rows, 16, cols), BF16),
             pltpu.VMEM((3, mid, 3 * mid), BF16),
             pltpu.VMEM((3, mid, 3 * mid), BF16),
-            pltpu.VMEM((mid, chans), BF16),
+            pltpu.VMEM((chans, mid), BF16),
             pltpu.VMEM((3, 3, outs, chans), BF16),
             pltpu.VMEM((3, chans, 3 * outs), BF16),
             [pltpu.VMEM((depth, cols), BF16) for depth in depths],
             [pltpu.VMEM((2, depth, cols), BF16) for depth in depths],
             pltpu.VMEM((8, 128), F32),
-            [pltpu.VMEM((sizes[axis], 8, 128), F32) for axis in AXES],
-            pltpu.VMEM((3 * share, chans), BF16),
-            pltpu.VMEM((3 * share, chans), F32),
-            pltpu.VMEM((3 * share, chans), BF16),
-            [slots(order) for order in orders],
-            small(4 * mid, BF16),
-            small(mid, F32),
+            whole_refs((8, 128), F32),
+            [split_refs(3 * outs) for _ in range(3)],
+            split_refs(4 * mid),
+            whole_refs((mid, chans), BF16),
             pltpu.SemaphoreType.DMA((copies,)),
             pltpu.SemaphoreType.DMA((copies,)),
+            pltpu.SemaphoreType.DMA((9,)),
         ],
         compiler_params=pltpu.CompilerParams(
             collective_id=1, has_side_effects=True, vmem_limit_bytes=60 * 1024 * 1024
@@ -520,9 +479,16 @@
         name="tile_step",
     )(
         x, anchor_labels[0], anchor_mask[0], spread, reduce_weight, spatial_weight,
-        expand_weight, class_weight,
+        expand_weight.T, class_weight,
     )
-    return loss.reshape(()), *grads
+    scale = scale.reshape(())
+    return (
+        loss.reshape(()),
+        small[:mid] * scale,
+        spatial * scale,
+        (small[mid:] * scale).T,
+        wide[:, :, :heads].astype(F32) * scale,
+    )
 
 
 def solution(mesh):

time: 92.1 us -> 79.4 us (0.86)
  Pallas kernels: 76.9 us -> 66.8 us
  local copies, waits for them, and re-layouts: 12.5 us -> 3.74 us
  other arithmetic: 0 us -> 6.09 us
    pallas_call x1, Pallas kernels: 76.9 us -> 66.8 us  [per_device(): pl.pallas_call(functools.partial(step_kernel, sizes, heads), out_shape=[j...]
    unnamed x6 -> x3, local copies, waits for them, and re-layouts: 12.5 us -> 3.74 us
    mul x0 -> x2, other arithmetic: none -> 3.94 us  [the longest x1 2.26 us: per_device(): spatial * scale]
    transpose x0 -> x1, other arithmetic: none -> 2.15 us  [per_device(): return (loss.reshape(()), small[:mid] * scale, spatial * scale, (small[mi...]
where the time goes in v4:
time: 79.4 us; the launch traced here: 79.1 us
  Pallas kernels  66.8 us (84%)
  other arithmetic  6.09 us (8%)
  local copies, waits for them, and re-layouts  3.74 us (5%)
  between operations  2.45 us (3%)
    pallas_call x1, Pallas kernels, per_device(): pl.pallas_call(functools.partial(step_kernel, sizes, heads), out_shape=[j...  66.8 us
    unnamed x3, local copies, waits for them, and re-layouts  3.74 us
    mul x1, other arithmetic, per_device(): spatial * scale  2.26 us
    transpose x1, other arithmetic, per_device(): return (loss.reshape(()), small[:mid] * scale, spatial * scale, (small[mi...  2.15 us
    mul x1, other arithmetic, per_device(): wide[:, :, :heads].astype(F32) * scale  1.68 us

profile of v4, /device:TPU:0, one launch (start us, length us, event | category | flops | bytes accessed | tf_op | source)
XLA Modules:
  0.0 79.1 jit_solution(14320716985373634578)
XLA Ops:
  0.6 3.7 %copy.15 = bf16[1,256,32,128]{3,1,2,0:T(8,128)(2,1)} copy(bf16[1,256,32,128]{3,2,1,0:T(8,128)(2,1)} %param.8) | data formatting | bytes 4194304 | tf_op args[0]
  4.4 66.8 %tile_step.1 = (f32[1,1]{1,0:T(1,128)}, f32[1,1]{1,0:T(1,128)}, f32[128,256]{1,0:T(8,128)}, f32[3,3,64,64]{3,2,1,0:T(8,128)}, bf16[3,3,144,256]{3,2,1,0:T(8,128)(2,1)}) custom-call(bf16[32,256,128]{2,1,0:T(8,128)(2,1)} %bitcast.12, s32[9,32,128]{2,1,0:T(8,128)} %bitcast.13, s32[9,32,128]{2,1,0:T(8,128)} %bitcast.14, ...), custom_call_target="tpu_custom_call" | custom-call | tf_op jit(solution)/shard_map/tile_step/pallas_call | solution.py:441
  71.2 0.0 copy-start
  71.2 2.2 %multiply_bitcast_fusion = (f32[256,64]{0,1:T(8,128)}, f32[64,256]{1,0:T(8,128)}) fusion(f32[128,256]{1,0:T(8,128)} %get-tuple-element.11, f32[]{:T(128)} %bitcast.6), kind=kLoop, calls=%fused_computation.3 | loop fusion | flops 32768 | bytes 262148 | tf_op jit(solution)/shard_map/transpose | solution.py:489
  73.4 2.3 %broadcast_multiply_fusion = f32[3,3,64,64]{3,2,1,0:T(8,128)} fusion(f32[3,3,64,64]{3,2,1,0:T(8,128)} %get-tuple-element.13, f32[]{:T(128)} %bitcast.6), kind=kLoop, calls=%fused_computation.2 | loop fusion | flops 36864 | bytes 294916 | tf_op jit(solution)/shard_map/mul | solution.py:488
  75.6 0.0 copy-done
  75.6 1.7 %convert_multiply_fusion = f32[3,3,135,256]{3,2,1,0:T(8,128)} fusion(f32[]{:T(128)} %bitcast.6, bf16[3,3,144,256]{3,2,1,0:T(8,128)(2,1)S(1)} %copy-done), kind=kLoop, calls=%fused_computation.1 | loop fusion | flops 622080 | bytes 1866244 | tf_op jit(solution)/shard_map/mul | solution.py:490
Async XLA Ops:
  71.2 4.4 %copy-start = (bf16[3,3,144,256]{3,2,1,0:T(8,128)(2,1)S(1)}, bf16[3,3,144,256]{3,2,1,0:T(8,128)(2,1)}, u32[]{:S(2)}) copy-start(bf16[3,3,144,256]{3,2,1,0:T(8,128)(2,1)} %get-tuple-element.14) | copy-start | bytes 1990660

commit v5 on v4

--- a/solution.py
+++ b/solution.py
@@ -10,8 +10,12 @@
 
 A = 9
 K = 15
-GROUP = 4
-WIDE = 8
+FIRST = (4, 1)
+BLOCK = (4, 2)
+DLOG = (2, 4)
+DSEC = (4, 1)
+DFIRST = 16
+WIDE = 16
 LOG2E = 1.4426950408889634
 LN2 = 0.6931471805599453
 F32 = jnp.float32
@@ -203,18 +207,25 @@
                 field[i, 2 * depth:, :],
             )
 
-    def conv(weight, field, at):
-        return sum(dot(weight(dy), cat(field, at + dy, GROUP)) for dy in range(3))
-
-    def sweep(body, between, init=0, halfway=None):
-        groups = rows // GROUP
-        carry = loop(2, lambda j, c: body(j * (groups - 1), c), init)
+    def conv(weight, field, at, count):
+        return sum(dot(weight(dy), cat(field, at + dy, count)) for dy in range(3))
+
+    def sweep(body, between, size, init=0, halfway=None):
+        count, runs = size
+        groups = rows // (count * runs)
+
+        def run(j, carry):
+            for u in range(runs):
+                carry = body((j * runs + u) * count, carry)
+            return carry
+
+        carry = loop(2, lambda j, c: run(j * (groups - 1), c), init)
         held = between()
         half = groups // 2 - 1
-        carry = loop(half, lambda j, c: body(j + 1, c), carry)
+        carry = loop(half, lambda j, c: run(j + 1, c), carry)
         if halfway is not None:
             halfway()
-        return held, loop(groups - 2 - half, lambda j, c: body(j + 1 + half, c), carry)
+        return held, loop(groups - 2 - half, lambda j, c: run(j + 1 + half, c), carry)
 
     fields = [(first, mid), (block, chans), (dlog, outs), (dsec, mid)]
     for n, (field, depth) in enumerate(fields):
@@ -228,11 +239,11 @@
     pl.semaphore_wait(barrier, len(across) + len(along))
 
     def make_first(i, c):
-        z = dot(wr_ref[...], cat(x_ref, i * GROUP, GROUP))
-        publish(0, first, mid, i * GROUP + 1, jnp.maximum(z, 0.0).astype(BF16))
+        z = dot(wr_ref[...], cat(x_ref, i, FIRST[0]))
+        publish(0, first, mid, i + 1, jnp.maximum(z, 0.0).astype(BF16))
         return c
 
-    held, _ = sweep(make_first, lambda: send_rows(0, first, mid))
+    held, _ = sweep(make_first, lambda: send_rows(0, first, mid), FIRST)
     for dy in range(3):
         for dx in range(3):
             ws_ref[dy, :, dx * mid:(dx + 1) * mid] = spatial_ref[dy, dx]
@@ -259,13 +270,13 @@
     widen(0, first, mid, held)
 
     def make_block(i, c):
-        s = jnp.maximum(conv(lambda dy: ws_ref[dy], first, i * GROUP), 0.0).astype(BF16)
-        spread_rows(second, i * GROUP, s)
-        b = jnp.maximum(cat(x_ref, i * GROUP, GROUP).astype(F32) + dot(we_ref[...], s), 0.0)
-        publish(1, block, chans, i * GROUP + 1, b.astype(BF16))
+        s = jnp.maximum(conv(lambda dy: ws_ref[dy], first, i, BLOCK[0]), 0.0).astype(BF16)
+        spread_rows(second, i, s)
+        b = jnp.maximum(cat(x_ref, i, BLOCK[0]).astype(F32) + dot(we_ref[...], s), 0.0)
+        publish(1, block, chans, i + 1, b.astype(BF16))
         return c
 
-    held, _ = sweep(make_block, lambda: send_rows(1, block, chans))
+    held, _ = sweep(make_block, lambda: send_rows(1, block, chans), BLOCK)
     held = send_strip(1, block, chans, held)
     widen(1, block, chans, held)
 
@@ -274,8 +285,8 @@
 
     def make_dlog(i, carry):
         total, count = carry
-        z = conv(class_rows, block, i * GROUP)
-        code = cat(code_ref, i * GROUP, GROUP)
+        z = conv(class_rows, block, i, DLOG[0])
+        code = cat(code_ref, i, DLOG[0])
         gap = dot(spread_ref[...], code)
         target = gap == 0.0
         alpha = jnp.where(target, 0.25, jnp.where(gap > 32.0, 0.0, 0.75))
@@ -288,16 +299,16 @@
         total = total + jnp.sum(scaled * soft, axis=0, keepdims=True)
         slope = scaled * ((2.0 * LN2 - 2.0 * LN2 * prob) * soft + prob)
         d = jnp.where(target, -slope, slope).astype(BF16)
-        publish(2, dlog, outs, i * GROUP + 1, d)
-        spread_rows(dzero, i * GROUP + 1, d)
+        publish(2, dlog, outs, i + 1, d)
+        spread_rows(dzero, i + 1, d)
         codes = code.astype(F32)
         row = lax.broadcasted_iota(jnp.int32, codes.shape, 0)
         hit = jnp.where((codes > 0.5) & (codes < 32.0) & (row < A), 1.0, 0.0)
         count = count + jnp.sum(hit, axis=0, keepdims=True)
         return total, count
 
-    zero = jnp.zeros((1, GROUP * cols), F32)
-    held, (total, count) = sweep(make_dlog, lambda: send_rows(2, dlog, outs), (zero, zero))
+    zero = jnp.zeros((1, DLOG[0] * cols), F32)
+    held, (total, count) = sweep(make_dlog, lambda: send_rows(2, dlog, outs), DLOG, (zero, zero))
     fold = lambda v: sum(v[:, k * 128:(k + 1) * 128] for k in range(v.shape[1] // 128))
     stat[0:1, :] = fold(total) * LN2
     stat[1:2, :] = fold(count)
@@ -329,21 +340,24 @@
         low, high = dx * chans, (dx + 1) * chans
         weight_sum(acc_c, dzero, block, low, high)
         send = big_refs[dx][0]
-        send[:3 * outs, :] = acc_c[...].astype(BF16)
+        for h in range(chans // 128):
+            send[h * 3 * outs:(h + 1) * 3 * outs, :] = acc_c[
+                :, h * 128:(h + 1) * 128
+            ].astype(BF16)
         bigs.append(reduce_split(big_refs[dx]))
         advance(bigs[dx])
     widen(2, dlog, outs, held)
 
     def make_dsec(i, c):
-        g = conv(lambda dy: wcb_ref[dy], dlog, i * GROUP)
-        b = cat(block, i * GROUP + 1, GROUP, chans, 2 * chans).astype(F32)
+        g = conv(lambda dy: wcb_ref[dy], dlog, i, DSEC[0])
+        b = cat(block, i + 1, DSEC[0], chans, 2 * chans).astype(F32)
         ds = jnp.where(b > 0.0, g, 0.0).astype(BF16)
-        s = cat(second, i * GROUP, GROUP)
+        s = cat(second, i, DSEC[0])
         acc_e[...] += dot_t(s, ds)
         h = dot(wet_ref[...], ds)
         d = jnp.where(s.astype(F32) > 0.0, h, 0.0).astype(BF16)
-        publish(3, dsec, mid, i * GROUP + 1, d)
-        spread_rows(dsec_zero, i * GROUP + 1, d)
+        publish(3, dsec, mid, i + 1, d)
+        spread_rows(dsec_zero, i + 1, d)
         return c
 
     def after_edges():
@@ -351,7 +365,7 @@
         advance(bigs[0], stats)
         return sent
 
-    held, _ = sweep(make_dsec, after_edges, halfway=lambda: advance(*bigs[1:]))
+    held, _ = sweep(make_dsec, after_edges, DSEC, halfway=lambda: advance(*bigs[1:]))
     held = send_strip(3, dsec, mid, held)
     advance(bigs[0], stats)
     weight_sum(acc_s, dsec_zero, first, 0, 3 * mid)
@@ -365,31 +379,36 @@
     advance(bigs[2])
 
     def make_dfirst(i, c):
-        g = conv(lambda dy: wsb_ref[dy], dsec, i * GROUP)
-        f = cat(first, i * GROUP + 1, GROUP, mid, 2 * mid).astype(F32)
+        g = conv(lambda dy: wsb_ref[dy], dsec, i, DFIRST)
+        f = cat(first, i + 1, DFIRST, mid, 2 * mid).astype(F32)
         df = jnp.where(f > 0.0, g, 0.0).astype(BF16)
-        acc_r[...] += dot_t(df, cat(x_ref, i * GROUP, GROUP))
+        acc_r[...] += dot_t(df, cat(x_ref, i, DFIRST))
         return c
 
-    loop(rows // GROUP, make_dfirst)
+    loop(rows // DFIRST, lambda j, c: make_dfirst(j * DFIRST, c))
 
     def place_tail(value):
         small_out[:mid, :] = value
 
     tail = reduce_whole(acc_r[...], *tail_refs, place_tail)
-    advance(tail, middle, *bigs)
-    outgoing = []
-    for dx in range(3):
-        for dy in range(3):
-            outgoing.append(pltpu.make_async_copy(
-                big_refs[dx][1].at[pl.ds(dy * outs, outs)], class_out.at[dy, dx],
-                osem.at[3 * dx + dy],
-            ))
-            outgoing[-1].start()
+    advance(tail)
     scale = 1.0 / jnp.sum(stat[1:2, :], axis=1, keepdims=True)
     scale_ref[...] = scale
     loss_ref[...] = jnp.sum(stat[0:1, :], axis=1, keepdims=True) * scale
-    advance(tail, middle)
+    advance(middle)
+    advance(tail)
+    outgoing = []
+    for dx in range(3):
+        advance(bigs[dx])
+        for h in range(chans // 128):
+            for dy in range(3):
+                at = (3 * h + dy) * outs
+                outgoing.append(pltpu.make_async_copy(
+                    big_refs[dx][1].at[pl.ds(at, outs)],
+                    class_out.at[dy, dx, :, pl.ds(h * 128, 128)], osem.at[len(outgoing)],
+                ))
+                outgoing[-1].start()
+    advance(middle)
     advance(middle)
     small_out[mid:, :] = mid_full[:mid, :].astype(F32)
     for dy in range(3):
@@ -422,11 +441,11 @@
     depths = (mid, chans, outs, mid)
     across = sizes["dp"] * sizes["col"]
 
-    def split_refs(need):
+    def split_refs(need, wide):
         piece = -(-need // (16 * across)) * 16
-        full = pltpu.VMEM((piece * across, chans), BF16)
+        full = pltpu.VMEM((piece * across, wide), BF16)
         return [full, full] + [
-            pltpu.VMEM((count, piece, chans), BF16) for count in (across, sizes["row"])
+            pltpu.VMEM((count, piece, wide), BF16) for count in (across, sizes["row"])
         ]
 
     def whole_refs(shape, kind):
@@ -466,15 +485,15 @@
             [pltpu.VMEM((2, depth, cols), BF16) for depth in depths],
             pltpu.VMEM((8, 128), F32),
             whole_refs((8, 128), F32),
-            [split_refs(3 * outs) for _ in range(3)],
-            split_refs(4 * mid),
+            [split_refs(3 * outs * chans // 128, 128) for _ in range(3)],
+            split_refs(4 * mid, chans),
             whole_refs((mid, chans), BF16),
             pltpu.SemaphoreType.DMA((copies,)),
             pltpu.SemaphoreType.DMA((copies,)),
-            pltpu.SemaphoreType.DMA((9,)),
+            pltpu.SemaphoreType.DMA((9 * chans // 128,)),
         ],
         compiler_params=pltpu.CompilerParams(
-            collective_id=1, has_side_effects=True, vmem_limit_bytes=60 * 1024 * 1024
+            collective_id=1, has_side_effects=True, vmem_limit_bytes=36 * 1024 * 1024
         ),
         name="tile_step",
     )(

time: 79.4 us -> 69.9 us (0.88)
  Pallas kernels: 66.8 us -> 60.3 us
  other arithmetic: 6.09 us -> 4.39 us
  local copies, waits for them, and re-layouts: 3.74 us -> 2.51 us
    pallas_call x1, Pallas kernels: 66.8 us -> 60.3 us  [per_device(): pl.pallas_call(functools.partial(step_kernel, sizes, heads), out_shape=[j...]
    unnamed x3 -> x15, local copies, waits for them, and re-layouts: 3.74 us -> 2.51 us
    mul x1, other arithmetic: 2.26 us -> 1.36 us  [per_device(): spatial * scale]
    transpose x1, other arithmetic: 2.15 us -> 1.28 us  [per_device(): return (loss.reshape(()), small[:mid] * scale, spatial * scale, (small[mi...]
where the time goes in v5:
time: 69.9 us; the launch traced here: 69.7 us
  Pallas kernels  60.3 us (86%)
  other arithmetic  4.39 us (6%)
  between operations  2.57 us (4%)
  local copies, waits for them, and re-layouts  2.51 us (4%)
    pallas_call x1, Pallas kernels, per_device(): pl.pallas_call(functools.partial(step_kernel, sizes, heads), out_shape=[j...  60.3 us
    unnamed x15, local copies, waits for them, and re-layouts  2.51 us
    mul x1, other arithmetic, per_device(): wide[:, :, :heads].astype(F32) * scale  1.75 us

profile of v5, /device:TPU:0, one launch (start us, length us, event | category | flops | bytes accessed | tf_op | source)
XLA Modules:
  0.0 69.7 jit_solution(1214708972333166522)
XLA Ops:
  0.6 0.0 copy-start
  0.6 0.0 copy-start.1
  0.7 0.0 copy-start.2
  0.7 0.0 copy-start.3
  0.7 0.0 copy-start.4
  0.7 0.0 copy-start.5
  0.7 0.0 copy-start.6
  0.7 2.5 %copy.15 = bf16[1,256,32,128]{3,1,2,0:T(8,128)(2,1)S(1)} copy(bf16[1,256,32,128]{3,2,1,0:T(8,128)(2,1)} %param.8) | data formatting | bytes 4194304 | tf_op args[0]
  3.2 0.0 copy-done
  3.2 0.0 copy-done.1
  3.2 0.0 copy-done.2
  3.2 0.0 copy-done.3
  3.2 0.0 copy-done.4
  3.2 0.0 copy-done.5
  3.2 0.0 copy-done.6
  3.3 60.3 %tile_step.1 = (f32[1,1]{1,0:T(1,128)}, f32[1,1]{1,0:T(1,128)}, f32[128,256]{1,0:T(8,128)S(1)}, f32[3,3,64,64]{3,2,1,0:T(8,128)S(1)}, bf16[3,3,144,256]{3,2,1,0:T(8,128)(2,1)S(1)}) custom-call(bf16[32,256,128]{2,1,0:T(8,128)(2,1)S(1)} %bitcast.12, s32[9,32,128]{2,1,0:T(8,128)S(1)} %bitcast.13, s32[9,32,128]{2,1,0:T(8,128)S(1)} %bitcast.14, ...), custom_call_target="tpu_custom_call" | custom-call | tf_op jit(solution)/shard_map/tile_step/pallas_call | solution.py:460
  63.5 1.3 %multiply_bitcast_fusion = (f32[256,64]{0,1:T(8,128)}, f32[64,256]{1,0:T(8,128)}) fusion(f32[128,256]{1,0:T(8,128)S(1)} %get-tuple-element.11, f32[]{:T(128)} %bitcast.6), kind=kLoop, calls=%fused_computation.3 | loop fusion | flops 32768 | bytes 262148 | tf_op jit(solution)/shard_map/transpose | solution.py:508
  64.8 1.4 %broadcast_multiply_fusion = f32[3,3,64,64]{3,2,1,0:T(8,128)} fusion(f32[3,3,64,64]{3,2,1,0:T(8,128)S(1)} %get-tuple-element.13, f32[]{:T(128)} %bitcast.6), kind=kLoop, calls=%fused_computation.2 | loop fusion | flops 36864 | bytes 294916 | tf_op jit(solution)/shard_map/mul | solution.py:507
  66.2 1.7 %convert_multiply_fusion = f32[3,3,135,256]{3,2,1,0:T(8,128)} fusion(f32[]{:T(128)} %bitcast.6, bf16[3,3,144,256]{3,2,1,0:T(8,128)(2,1)S(1)} %get-tuple-element.14), kind=kLoop, calls=%fused_computation.1 | loop fusion | flops 622080 | bytes 1866244 | tf_op jit(solution)/shard_map/mul | solution.py:509
Async XLA Ops:
  0.6 2.6 %copy-start = (bf16[3,3,135,256]{3,2,1,0:T(8,128)(2,1)S(1)}, bf16[3,3,135,256]{3,2,1,0:T(8,128)(2,1)}, u32[]{:S(2)}) copy-start(bf16[3,3,135,256]{3,2,1,0:T(8,128)(2,1)} %class_ref.1) | copy-start | bytes 1866244
  0.6 2.6 %copy-start.1 = (s32[1,9,32,128]{3,2,1,0:T(8,128)S(1)}, s32[1,9,32,128]{3,2,1,0:T(8,128)}, u32[]{:S(2)}) copy-start(s32[1,9,32,128]{3,2,1,0:T(8,128)} %param.13) | copy-start | bytes 442372
  0.7 2.6 %copy-start.2 = (s32[1,9,32,128]{3,2,1,0:T(8,128)S(1)}, s32[1,9,32,128]{3,2,1,0:T(8,128)}, u32[]{:S(2)}) copy-start(s32[1,9,32,128]{3,2,1,0:T(8,128)} %param.14) | copy-start | bytes 442372
  0.7 2.6 %copy-start.3 = (bf16[3,3,64,64]{3,2,1,0:T(8,128)(2,1)S(1)}, bf16[3,3,64,64]{3,2,1,0:T(8,128)(2,1)}, u32[]{:S(2)}) copy-start(bf16[3,3,64,64]{3,2,1,0:T(8,128)(2,1)} %spatial_ref.1) | copy-start | bytes 221188
  0.7 2.6 %copy-start.4 = (bf16[144,16]{1,0:T(8,128)(2,1)S(1)}, bf16[144,16]{1,0:T(8,128)(2,1)}, u32[]{:S(2)}) copy-start(bf16[144,16]{1,0:T(8,128)(2,1)} %constant.2.clone.spread_ref) | copy-start | bytes 13828
  0.7 2.6 %copy-start.5 = (bf16[64,256]{1,0:T(8,128)(2,1)S(1)}, bf16[64,256]{1,0:T(8,128)(2,1)}, u32[]{:S(2)}) copy-start(bf16[64,256]{1,0:T(8,128)(2,1)} %wr_ref.1) | copy-start | bytes 98308
  0.7 2.6 %copy-start.6 = (bf16[256,64]{0,1:T(8,128)(2,1)S(1)}, bf16[256,64]{0,1:T(8,128)(2,1)}, u32[]{:S(2)}) copy-start(bf16[256,64]{0,1:T(8,128)(2,1)} %param.11) | copy-start | bytes 98308

commit v6 on v5

--- a/solution.py
+++ b/solution.py
@@ -34,10 +34,10 @@
 def step_kernel(
     sizes, heads,
     x_ref, label_ref, mask_ref, spread_ref, wr_ref, spatial_ref, wet_ref, class_ref,
-    loss_ref, scale_ref, small_out, spatial_out, class_out,
+    small_out, spatial_out, class_out,
     first, second, block, dlog, dzero, dsec, dsec_zero, acc_c, acc_s, acc_e, acc_r,
     code_ref, ws_ref, wsb_ref, we_ref, wc_ref, wcb_ref, strips, got,
-    stat, stat_slots, big_refs, mid_refs, tail_refs, ssem, rsem, osem,
+    stat, stat_slots, big_refs, mid_refs, tail_refs, ssem, rsem,
 ):
     rows, chans, cols = x_ref.shape
     mid = wr_ref.shape[0]
@@ -104,13 +104,13 @@
         return copies
 
     def reduce_whole(value, plane_slots, row_slots, store):
-        copies = share_all(plane_slots, value, across, place(me))
+        copies = share_all(row_slots, value, along, me["row"])
         yield
         settle(copies)
-        copies = share_all(row_slots, total_of(plane_slots), along, me["row"])
+        copies = share_all(plane_slots, total_of(row_slots), across, place(me))
         yield
         settle(copies)
-        store(total_of(row_slots))
+        store(total_of(plane_slots))
 
     def reduce_split(refs):
         send, full, plane_slots, row_slots = refs
@@ -393,31 +393,28 @@
     tail = reduce_whole(acc_r[...], *tail_refs, place_tail)
     advance(tail)
     scale = 1.0 / jnp.sum(stat[1:2, :], axis=1, keepdims=True)
-    scale_ref[...] = scale
-    loss_ref[...] = jnp.sum(stat[0:1, :], axis=1, keepdims=True) * scale
+    loss = jnp.sum(stat[0:1, :], axis=1, keepdims=True) * scale
     advance(middle)
     advance(tail)
-    outgoing = []
     for dx in range(3):
         advance(bigs[dx])
         for h in range(chans // 128):
             for dy in range(3):
                 at = (3 * h + dy) * outs
-                outgoing.append(pltpu.make_async_copy(
-                    big_refs[dx][1].at[pl.ds(at, outs)],
-                    class_out.at[dy, dx, :, pl.ds(h * 128, 128)], osem.at[len(outgoing)],
-                ))
-                outgoing[-1].start()
+                class_out[dy, dx, :, h * 128:(h + 1) * 128] = (
+                    big_refs[dx][1][at:at + outs, :].astype(F32) * scale
+                )
     advance(middle)
     advance(middle)
-    small_out[mid:, :] = mid_full[:mid, :].astype(F32)
+    small_out[mid:2 * mid, :] = mid_full[:mid, :].astype(F32) * scale
+    small_out[2 * mid:, :] = jnp.broadcast_to(loss, (8, chans))
     for dy in range(3):
-        part = mid_full[(dy + 1) * mid:(dy + 2) * mid, :].astype(F32)
+        part = mid_full[(dy + 1) * mid:(dy + 2) * mid, :].astype(F32) * scale
         for dx in range(3):
             spatial_out[dy, dx] = part[:, dx * mid:(dx + 1) * mid]
+    spatial_out[3] = jnp.zeros(spatial_out.shape[1:], F32)
     advance(tail)
-    for copy in outgoing:
-        copy.wait()
+    small_out[:mid, :] = small_out[:mid, :] * scale
 
 
 def per_device(
@@ -453,16 +450,14 @@
 
     copies = 16 + 6 * (across - 1) + 4 * (across - 1) + 6 * (sizes["row"] - 1)
     outputs = [
-        ((1, 1), F32), ((1, 1), F32), ((2 * mid, chans), F32), ((3, 3, mid, mid), F32),
-        ((3, 3, outs, chans), BF16),
+        ((2 * mid + 8, chans), F32), ((4, 3, mid, mid), F32), ((3, 3, outs, chans), F32)
     ]
 
-    loss, scale, small, spatial, wide = pl.pallas_call(
+    small, spatial, wide = pl.pallas_call(
         functools.partial(step_kernel, sizes, heads),
         out_shape=[jax.ShapeDtypeStruct(*output) for output in outputs],
         in_specs=[pl.BlockSpec(memory_space=pltpu.VMEM)] * 8,
-        out_specs=[pl.BlockSpec(memory_space=pltpu.VMEM)] * 4
-        + [pl.BlockSpec(memory_space=pl.ANY)],
+        out_specs=[pl.BlockSpec(memory_space=pltpu.VMEM)] * 3,
         scratch_shapes=[
             pltpu.VMEM((rows + 2, 3 * mid, cols), BF16),
             pltpu.VMEM((rows, mid, cols), BF16),
@@ -490,7 +485,6 @@
             whole_refs((mid, chans), BF16),
             pltpu.SemaphoreType.DMA((copies,)),
             pltpu.SemaphoreType.DMA((copies,)),
-            pltpu.SemaphoreType.DMA((9 * chans // 128,)),
         ],
         compiler_params=pltpu.CompilerParams(
             collective_id=1, has_side_effects=True, vmem_limit_bytes=36 * 1024 * 1024
@@ -500,13 +494,8 @@
         x, anchor_labels[0], anchor_mask[0], spread, reduce_weight, spatial_weight,
         expand_weight.T, class_weight,
     )
-    scale = scale.reshape(())
     return (
-        loss.reshape(()),
-        small[:mid] * scale,
-        spatial * scale,
-        (small[mid:] * scale).T,
-        wide[:, :, :heads].astype(F32) * scale,
+        small[2 * mid, 0], small[:mid], spatial[:3], small[mid:2 * mid].T, wide[:, :, :heads]
     )
 
 

time: 69.9 us -> 63.4 us (0.907)
  other arithmetic: 4.39 us -> 0 us
  Pallas kernels: 60.3 us -> 56.9 us
  local copies, waits for them, and re-layouts: 2.51 us -> 5.55 us
  between operations: 2.57 us -> 0.76 us
    pallas_call x1, Pallas kernels: 60.3 us -> 56.9 us  [per_device(): pl.pallas_call(functools.partial(step_kernel, sizes, heads), out_shape=[j...]
    mul x2 -> x0, other arithmetic: 3.11 us -> none  [the longest x1 1.75 us: per_device(): wide[:, :, :heads].astype(F32) * scale]
    slice x0 -> x3, local copies, waits for them, and re-layouts: none -> 2.38 us  [the longest x1 1.14 us: per_device(): wide[:, :, :heads]]
    transpose x1 -> x0, other arithmetic: 1.28 us -> none  [per_device(): return (loss.reshape(()), small[:mid] * scale, spatial * scale, (small[mi...]
where the time goes in v6:
time: 63.4 us; the launch traced here: 63.2 us
  Pallas kernels  56.9 us (90%)
  local copies, waits for them, and re-layouts  5.55 us (9%)
  between operations  0.76 us (1%)
    pallas_call x1, Pallas kernels, per_device(): pl.pallas_call(functools.partial(step_kernel, sizes, heads), out_shape=[j...  56.9 us
    unnamed x15, local copies, waits for them, and re-layouts  2.51 us

profile of v6, /device:TPU:0, one launch (start us, length us, event | category | flops | bytes accessed | tf_op | source)
XLA Modules:
  0.0 63.2 jit_solution(12724558995221574433)
XLA Ops:
  0.6 0.0 copy-start
  0.6 0.0 copy-start.1
  0.7 0.0 copy-start.2
  0.7 0.0 copy-start.3
  0.7 0.0 copy-start.4
  0.7 0.0 copy-start.5
  0.7 0.0 copy-start.6
  0.7 2.5 %copy.15 = bf16[1,256,32,128]{3,1,2,0:T(8,128)(2,1)S(1)} copy(bf16[1,256,32,128]{3,2,1,0:T(8,128)(2,1)} %param.8) | data formatting | bytes 4194304 | tf_op args[0]
  3.2 0.0 copy-done
  3.2 0.0 copy-done.1
  3.2 0.0 copy-done.2
  3.2 0.0 copy-done.3
  3.2 0.0 copy-done.4
  3.2 0.0 copy-done.5
  3.2 0.0 copy-done.6
  3.3 56.9 %tile_step.1 = (f32[136,256]{1,0:T(8,128)S(1)}, f32[4,3,64,64]{3,2,1,0:T(8,128)S(1)}, f32[3,3,144,256]{3,2,1,0:T(8,128)S(1)}) custom-call(bf16[32,256,128]{2,1,0:T(8,128)(2,1)S(1)} %bitcast.11, s32[9,32,128]{2,1,0:T(8,128)S(1)} %bitcast.12, s32[9,32,128]{2,1,0:T(8,128)S(1)} %bitcast.13, bf16[144,16]{1,0:T(8,128)(2,1)S(1)} %copy-done.4, ...), custom_call_target="tpu_custom_call" | custom-call | tf_op jit(solution)/shard_map/tile_step/pallas_call | solution.py:456
  60.2 0.5 slice.15
  60.7 0.7 %slice.17 = f32[3,3,64,64]{3,2,1,0:T(8,128)} slice(f32[4,3,64,64]{3,2,1,0:T(8,128)S(1)} %get-tuple-element.9), slice={[0:3], [0:3], [0:64], [0:64]} | slice | bytes 294912 | tf_op jit(solution)/shard_map/slice | solution.py:498
  61.4 0.7 %slice_bitcast_fusion = (f32[256,64]{0,1:T(8,128)}, f32[64,256]{1,0:T(8,128)}) fusion(f32[136,256]{1,0:T(8,128)S(1)} %get-tuple-element.8), kind=kLoop, calls=%fused_computation.1 | loop fusion | bytes 262144 | tf_op jit(solution)/shard_map/transpose | solution.py:498
  62.1 1.1 %slice.19 = f32[3,3,135,256]{3,2,1,0:T(8,128)} slice(f32[3,3,144,256]{3,2,1,0:T(8,128)S(1)} %get-tuple-element.10), slice={[0:3], [0:3], [0:135], [0:256]} | slice | bytes 2488320 | tf_op jit(solution)/shard_map/slice | solution.py:498
Async XLA Ops:
  0.6 2.6 %copy-start = (bf16[3,3,135,256]{3,2,1,0:T(8,128)(2,1)S(1)}, bf16[3,3,135,256]{3,2,1,0:T(8,128)(2,1)}, u32[]{:S(2)}) copy-start(bf16[3,3,135,256]{3,2,1,0:T(8,128)(2,1)} %class_ref.1) | copy-start | bytes 1866244
  0.6 2.6 %copy-start.1 = (s32[1,9,32,128]{3,2,1,0:T(8,128)S(1)}, s32[1,9,32,128]{3,2,1,0:T(8,128)}, u32[]{:S(2)}) copy-start(s32[1,9,32,128]{3,2,1,0:T(8,128)} %param.13) | copy-start | bytes 442372
  0.7 2.6 %copy-start.2 = (s32[1,9,32,128]{3,2,1,0:T(8,128)S(1)}, s32[1,9,32,128]{3,2,1,0:T(8,128)}, u32[]{:S(2)}) copy-start(s32[1,9,32,128]{3,2,1,0:T(8,128)} %param.14) | copy-start | bytes 442372
  0.7 2.6 %copy-start.3 = (bf16[3,3,64,64]{3,2,1,0:T(8,128)(2,1)S(1)}, bf16[3,3,64,64]{3,2,1,0:T(8,128)(2,1)}, u32[]{:S(2)}) copy-start(bf16[3,3,64,64]{3,2,1,0:T(8,128)(2,1)} %spatial_ref.1) | copy-start | bytes 221188
  0.7 2.6 %copy-start.4 = (bf16[144,16]{1,0:T(8,128)(2,1)S(1)}, bf16[144,16]{1,0:T(8,128)(2,1)}, u32[]{:S(2)}) copy-start(bf16[144,16]{1,0:T(8,128)(2,1)} %constant.2.clone.spread_ref) | copy-start | bytes 13828
  0.7 2.6 %copy-start.5 = (bf16[64,256]{1,0:T(8,128)(2,1)S(1)}, bf16[64,256]{1,0:T(8,128)(2,1)}, u32[]{:S(2)}) copy-start(bf16[64,256]{1,0:T(8,128)(2,1)} %wr_ref.1) | copy-start | bytes 98308
  0.7 2.6 %copy-start.6 = (bf16[256,64]{0,1:T(8,128)(2,1)S(1)}, bf16[256,64]{0,1:T(8,128)(2,1)}, u32[]{:S(2)}) copy-start(bf16[256,64]{0,1:T(8,128)(2,1)} %param.11) | copy-start | bytes 98308

commit v7 on v6

--- a/solution.py
+++ b/solution.py
@@ -197,15 +197,13 @@
         for wait in held:
             wait()
         lane = lax.broadcasted_iota(jnp.int32, (depth, cols), 1)
-        before, after = got[n][0], got[n][1]
+        both = jnp.where(
+            lane % 2 == 1, pltpu.roll(got[n][0], 1, 1), pltpu.roll(got[n][1], cols - 1, 1)
+        )
         for i in range(rows + 2):
-            field[i, :depth, :] = jnp.where(
-                lane == 0, pltpu.roll(before, (cols - 2 * i) % cols, 1), field[i, :depth, :]
-            )
-            field[i, 2 * depth:, :] = jnp.where(
-                lane == cols - 1, pltpu.roll(after, (cols - 2 - 2 * i) % cols, 1),
-                field[i, 2 * depth:, :],
-            )
+            ends = pltpu.roll(both, (cols - 1 - 2 * i) % cols, 1)
+            field[i, :depth, :] = jnp.where(lane == 0, ends, field[i, :depth, :])
+            field[i, 2 * depth:, :] = jnp.where(lane == cols - 1, ends, field[i, 2 * depth:, :])
 
     def conv(weight, field, at, count):
         return sum(dot(weight(dy), cat(field, at + dy, count)) for dy in range(3))
@@ -289,16 +287,15 @@
         code = cat(code_ref, i, DLOG[0])
         gap = dot(spread_ref[...], code)
         target = gap == 0.0
-        alpha = jnp.where(target, 0.25, jnp.where(gap > 32.0, 0.0, 0.75))
-        z = z * LOG2E
-        u = jnp.where(target, -z, z)
+        alpha = jnp.where(target, -0.25, jnp.where(gap > 32.0, 0.0, 0.75))
+        u = z * jnp.where(target, -LOG2E, LOG2E)
         e = jnp.exp2(-jnp.abs(u))
         soft = jnp.maximum(u, 0.0) + jnp.log2(1.0 + e)
         prob = jnp.exp2(u - soft)
-        scaled = alpha * prob * prob
-        total = total + jnp.sum(scaled * soft, axis=0, keepdims=True)
-        slope = scaled * ((2.0 * LN2 - 2.0 * LN2 * prob) * soft + prob)
-        d = jnp.where(target, -slope, slope).astype(BF16)
+        scaled = alpha * (prob * prob)
+        terms = jnp.abs(scaled * soft)
+        total = total + sum(terms[8 * k:8 * k + 8] for k in range(outs // 8))
+        d = (scaled * ((2.0 * LN2 - 2.0 * LN2 * prob) * soft + prob)).astype(BF16)
         publish(2, dlog, outs, i + 1, d)
         spread_rows(dzero, i + 1, d)
         codes = code.astype(F32)
@@ -308,7 +305,11 @@
         return total, count
 
     zero = jnp.zeros((1, DLOG[0] * cols), F32)
-    held, (total, count) = sweep(make_dlog, lambda: send_rows(2, dlog, outs), DLOG, (zero, zero))
+    zeros = jnp.zeros((8, DLOG[0] * cols), F32)
+    held, (total, count) = sweep(
+        make_dlog, lambda: send_rows(2, dlog, outs), DLOG, (zeros, zero)
+    )
+    total = jnp.sum(total, axis=0, keepdims=True)
     fold = lambda v: sum(v[:, k * 128:(k + 1) * 128] for k in range(v.shape[1] // 128))
     stat[0:1, :] = fold(total) * LN2
     stat[1:2, :] = fold(count)
@@ -396,6 +397,7 @@
     loss = jnp.sum(stat[0:1, :], axis=1, keepdims=True) * scale
     advance(middle)
     advance(tail)
+    advance(middle)
     for dx in range(3):
         advance(bigs[dx])
         for h in range(chans // 128):
@@ -404,7 +406,6 @@
                 class_out[dy, dx, :, h * 128:(h + 1) * 128] = (
                     big_refs[dx][1][at:at + outs, :].astype(F32) * scale
                 )
-    advance(middle)
     advance(middle)
     small_out[mid:2 * mid, :] = mid_full[:mid, :].astype(F32) * scale
     small_out[2 * mid:, :] = jnp.broadcast_to(loss, (8, chans))

time: 63.4 us -> 61.9 us (0.976)
  Pallas kernels: 56.9 us -> 55.5 us
    pallas_call x1, Pallas kernels: 56.9 us -> 55.5 us  [per_device(): pl.pallas_call(functools.partial(step_kernel, sizes, heads), out_shape=[j...]
where the time goes in v7:
time: 61.9 us; the launch traced here: 61.8 us
  Pallas kernels  55.5 us (90%)
  local copies, waits for them, and re-layouts  5.55 us (9%)
  between operations  0.76 us (1%)
    pallas_call x1, Pallas kernels, per_device(): pl.pallas_call(functools.partial(step_kernel, sizes, heads), out_shape=[j...  55.5 us
    unnamed x15, local copies, waits for them, and re-layouts  2.51 us

profile of v7, /device:TPU:0, one launch (start us, length us, event | category | flops | bytes accessed | tf_op | source)
XLA Modules:
  0.0 61.8 jit_solution(9075497742503652795)
XLA Ops:
  0.6 0.0 copy-start
  0.6 0.0 copy-start.1
  0.7 0.0 copy-start.2
  0.7 0.0 copy-start.3
  0.7 0.0 copy-start.4
  0.7 0.0 copy-start.5
  0.7 0.0 copy-start.6
  0.7 2.5 %copy.15 = bf16[1,256,32,128]{3,1,2,0:T(8,128)(2,1)S(1)} copy(bf16[1,256,32,128]{3,2,1,0:T(8,128)(2,1)} %param.8) | data formatting | bytes 4194304 | tf_op args[0]
  3.2 0.0 copy-done
  3.2 0.0 copy-done.1
  3.2 0.0 copy-done.2
  3.2 0.0 copy-done.3
  3.2 0.0 copy-done.4
  3.2 0.0 copy-done.5
  3.2 0.0 copy-done.6
  3.3 55.5 %tile_step.1 = (f32[136,256]{1,0:T(8,128)S(1)}, f32[4,3,64,64]{3,2,1,0:T(8,128)S(1)}, f32[3,3,144,256]{3,2,1,0:T(8,128)S(1)}) custom-call(bf16[32,256,128]{2,1,0:T(8,128)(2,1)S(1)} %bitcast.11, s32[9,32,128]{2,1,0:T(8,128)S(1)} %bitcast.12, s32[9,32,128]{2,1,0:T(8,128)S(1)} %bitcast.13, bf16[144,16]{1,0:T(8,128)(2,1)S(1)} %copy-done.4, ...), custom_call_target="tpu_custom_call" | custom-call | tf_op jit(solution)/shard_map/tile_step/pallas_call | solution.py:457
  58.7 0.5 slice.15
  59.3 0.7 %slice.17 = f32[3,3,64,64]{3,2,1,0:T(8,128)} slice(f32[4,3,64,64]{3,2,1,0:T(8,128)S(1)} %get-tuple-element.9), slice={[0:3], [0:3], [0:64], [0:64]} | slice | bytes 294912 | tf_op jit(solution)/shard_map/slice | solution.py:499
  60.0 0.7 %slice_bitcast_fusion = (f32[256,64]{0,1:T(8,128)}, f32[64,256]{1,0:T(8,128)}) fusion(f32[136,256]{1,0:T(8,128)S(1)} %get-tuple-element.8), kind=kLoop, calls=%fused_computation.1 | loop fusion | bytes 262144 | tf_op jit(solution)/shard_map/transpose | solution.py:499
  60.6 1.1 %slice.19 = f32[3,3,135,256]{3,2,1,0:T(8,128)} slice(f32[3,3,144,256]{3,2,1,0:T(8,128)S(1)} %get-tuple-element.10), slice={[0:3], [0:3], [0:135], [0:256]} | slice | bytes 2488320 | tf_op jit(solution)/shard_map/slice | solution.py:499
Async XLA Ops:
  0.6 2.6 %copy-start = (bf16[3,3,135,256]{3,2,1,0:T(8,128)(2,1)S(1)}, bf16[3,3,135,256]{3,2,1,0:T(8,128)(2,1)}, u32[]{:S(2)}) copy-start(bf16[3,3,135,256]{3,2,1,0:T(8,128)(2,1)} %class_ref.1) | copy-start | bytes 1866244
  0.6 2.6 %copy-start.1 = (s32[1,9,32,128]{3,2,1,0:T(8,128)S(1)}, s32[1,9,32,128]{3,2,1,0:T(8,128)}, u32[]{:S(2)}) copy-start(s32[1,9,32,128]{3,2,1,0:T(8,128)} %param.13) | copy-start | bytes 442372
  0.7 2.6 %copy-start.2 = (s32[1,9,32,128]{3,2,1,0:T(8,128)S(1)}, s32[1,9,32,128]{3,2,1,0:T(8,128)}, u32[]{:S(2)}) copy-start(s32[1,9,32,128]{3,2,1,0:T(8,128)} %param.14) | copy-start | bytes 442372
  0.7 2.6 %copy-start.3 = (bf16[3,3,64,64]{3,2,1,0:T(8,128)(2,1)S(1)}, bf16[3,3,64,64]{3,2,1,0:T(8,128)(2,1)}, u32[]{:S(2)}) copy-start(bf16[3,3,64,64]{3,2,1,0:T(8,128)(2,1)} %spatial_ref.1) | copy-start | bytes 221188
  0.7 2.6 %copy-start.4 = (bf16[144,16]{1,0:T(8,128)(2,1)S(1)}, bf16[144,16]{1,0:T(8,128)(2,1)}, u32[]{:S(2)}) copy-start(bf16[144,16]{1,0:T(8,128)(2,1)} %constant.2.clone.spread_ref) | copy-start | bytes 13828
  0.7 2.6 %copy-start.5 = (bf16[64,256]{1,0:T(8,128)(2,1)S(1)}, bf16[64,256]{1,0:T(8,128)(2,1)}, u32[]{:S(2)}) copy-start(bf16[64,256]{1,0:T(8,128)(2,1)} %wr_ref.1) | copy-start | bytes 98308
  0.7 2.6 %copy-start.6 = (bf16[256,64]{0,1:T(8,128)(2,1)S(1)}, bf16[256,64]{0,1:T(8,128)(2,1)}, u32[]{:S(2)}) copy-start(bf16[256,64]{0,1:T(8,128)(2,1)} %param.11) | copy-start | bytes 98308
